TPU v7x, 32 devices: a whole 2x2x4 slice. The times are simulated.
32 devices in a mesh: dp: 2 (over core), fsdp: 16 (over z, y, x).
Axes of the slice: x: 2, y: 2, z: 4, core: 2. Of those that a mesh axis runs over, the one named last changes fastest.
Arguments:
- images_in: bfloat16 [32, 22, 22, 768], P(('dp', 'fsdp')), may hold values from -6 to 6
- cotangent: bfloat16 [32, 22, 22, 768], P(('dp', 'fsdp')), may hold values from -6 to 6
- master: float32 [55936, 128], P('fsdp'), may hold values from -2 to 2
- moment: float32 [55936, 128], P('fsdp'), may hold values from -384 to 384
- second: float32 [55936, 128], P('fsdp'), may hold values from 774.4 to 30976
- owner: int32 [37212], replicated, may hold values from 0 to 15, as said below
- offset: int32 [37212], replicated, may hold values from 0 to 3495
Outputs:
- input_grad: bfloat16 [32, 22, 22, 768], P(('dp', 'fsdp'))
- new_master: float32 [55936, 128], P('fsdp')
- new_moment: float32 [55936, 128], P('fsdp')
- new_second: float32 [55936, 128], P('fsdp')
Inputs may be any that keep to these rules, and one draw needn't show every extreme that they name: Distinct rows r give distinct slots owner[r] * 3496 + offset[r]. The rows of one owner form one run of consecutive rows, with offsets 0, 1, 2 and so on along it; every owner holds at least one row, and one owner holds exactly 3496.
All inputs are finite; a program needn't handle non-finite values.
Results may differ from a plain program's by a relative error of at most 0.0055.
Values may be sent and summed in bfloat16 or wider, within the bound.
No kernel may reach another device: no remote copies, remote signals or barrier semaphores. Data moves between devices by JAX's collectives and lax.ppermute only.
A program may use at most 128 MiB of HBM per device.

v0:
```python
import math

import jax
import jax.numpy as jnp
from jax import lax
from jax.sharding import PartitionSpec as P

FF = 3072
KSIZE = 7


ROOT_HALF = 0.7071067811865476
DENSITY = 0.3989422804014327
LEARNING = 0.001
DECAY = 0.05
BETA_ONE = 0.9
BETA_TWO = 0.95
FIRST_FIX = 0.9999734386011124
SECOND_FIX = 0.994079470779666


def split_params(flat, widths, hidden, kernel):
    values = flat.reshape(-1)
    shapes = [
        (kernel, kernel, widths),
        (widths,),
        (widths,),
        (widths,),
        (widths, hidden),
        (hidden,),
        (hidden, widths),
        (widths,),
        (widths,),
    ]
    pieces = []
    start = 0
    for shape in shapes:
        count = math.prod(shape)
        pieces.append(values[start : start + count].reshape(shape))
        start = start + count
    return pieces


def conv_norm(window, depth_kernel, depth_bias, norm_gain, norm_shift):
    reach = depth_kernel.shape[0] // 2
    kernel = depth_kernel.reshape(
        depth_kernel.shape[0], depth_kernel.shape[1], 1, depth_kernel.shape[2]
    )
    mixed = (
        lax.conv_general_dilated(
            window[None],
            kernel,
            (1, 1),
            ((0, 0), (reach, reach)),
            dimension_numbers=("NHWC", "HWIO", "NHWC"),
            feature_group_count=window.shape[-1],
            precision=lax.Precision.HIGHEST,
        )[0]
        + depth_bias
    )
    centre = jnp.mean(mixed, -1, keepdims=True)
    centred = mixed - centre
    spread = jnp.mean(centred * centred, -1, keepdims=True)
    return centred * lax.rsqrt(spread + 1e-06) * norm_gain + norm_shift


def image_pass(window, cot_image, params):
    (
        depth_kernel,
        depth_bias,
        norm_gain,
        norm_shift,
        weight_in,
        bias_in,
        weight_out,
        bias_out,
        layer_scale,
    ) = params
    single = jnp.float32
    widths = window.shape[-1]
    normed, pullback = jax.vjp(
        conv_norm,
        window.astype(single),
        depth_kernel.astype(single),
        depth_bias.astype(single),
        norm_gain.astype(single),
        norm_shift.astype(single),
    )
    normed_low = normed.astype(jnp.bfloat16).reshape(-1, widths)
    before = jnp.dot(normed_low, weight_in, preferred_element_type=single) + bias_in.astype(single)
    activated = (before * 0.5 * (1.0 + lax.erf(before * ROOT_HALF))).astype(jnp.bfloat16)
    branch = jnp.dot(activated, weight_out, preferred_element_type=single) + bias_out.astype(single)
    cot_flat = cot_image.reshape(-1, widths).astype(single)
    branch_grad = (layer_scale.astype(single) * cot_flat).astype(jnp.bfloat16)
    grad_scale = jnp.sum(cot_flat * branch, 0)
    grad_bias_out = jnp.sum(branch_grad.astype(single), 0)
    grad_weight_out = lax.dot_general(
        activated, branch_grad, (((0,), (0,)), ((), ())), preferred_element_type=single
    )
    activated_grad = lax.dot_general(
        branch_grad, weight_out, (((1,), (1,)), ((), ())), preferred_element_type=single
    )
    slope = (
        0.5 * (1.0 + lax.erf(before * ROOT_HALF))
        + before * jnp.exp(-0.5 * before * before) * DENSITY
    )
    before_grad = (activated_grad * slope).astype(jnp.bfloat16)
    grad_bias_in = jnp.sum(before_grad.astype(single), 0)
    grad_weight_in = lax.dot_general(
        normed_low, before_grad, (((0,), (0,)), ((), ())), preferred_element_type=single
    )
    normed_grad = lax.dot_general(
        before_grad, weight_in, (((1,), (1,)), ((), ())), preferred_element_type=single
    )
    window_grad, grad_kernel, grad_bias, grad_gain, grad_shift = pullback(
        normed_grad.reshape(normed.shape)
    )
    lower = jnp.bfloat16
    small_term = jnp.concatenate(
        [
            grad_kernel.reshape(-1).astype(lower),
            grad_bias.astype(lower),
            grad_gain.astype(lower),
            grad_shift.astype(lower),
        ]
    ).reshape(-1, 128)
    large_term = jnp.concatenate(
        [
            grad_weight_in.reshape(-1).astype(lower),
            grad_bias_in.astype(lower),
            grad_weight_out.reshape(-1).astype(lower),
            grad_bias_out.astype(lower),
            grad_scale.astype(lower),
        ]
    ).reshape(-1, 128)
    return (small_term, large_term, window_grad)


def adam_update(gradient, weights, first, second_moment):
    first_new = BETA_ONE * first + (1.0 - BETA_ONE) * gradient
    second_new = BETA_TWO * second_moment + (1.0 - BETA_TWO) * gradient * gradient
    update = first_new / FIRST_FIX / (jnp.sqrt(second_new / SECOND_FIX) + 1e-08)
    weights_new = weights * (1.0 - LEARNING * DECAY) - LEARNING * update
    return (weights_new, first_new, second_new)


def per_device(images_in, cotangent, master, moment, second, owner, offset):
    widths = images_in.shape[-1]
    reach = KSIZE // 2
    fsdp_count = lax.axis_size("fsdp")
    replica_count = lax.axis_size("dp")
    bucket = master.shape[0]
    place = owner * bucket + offset
    lowered = master.astype(jnp.bfloat16)
    portion = bucket // replica_count
    mine = lax.dynamic_slice_in_dim(lowered, lax.axis_index("dp") * portion, portion, 0)
    gathered = lax.all_gather(mine, ("dp", "fsdp"), axis=0, tiled=True)
    lookup = offset // portion * (fsdp_count * portion) + owner * portion + offset % portion
    flat = jnp.take(gathered, lookup, axis=0)
    params = split_params(flat, widths, FF, KSIZE)
    own_rows = images_in[0]
    blank = jnp.zeros((reach,) + own_rows.shape[1:], own_rows.dtype)
    extended = jnp.concatenate([blank, own_rows, blank], 0)
    small_term, large_term, window_grad = image_pass(extended, cotangent[0], params)
    interior = window_grad[reach : reach + own_rows.shape[0]]
    input_grad = (cotangent[0].astype(jnp.float32) + interior).astype(jnp.bfloat16)[None]
    slots = jnp.zeros((fsdp_count * bucket, 128), jnp.bfloat16)
    slots = slots.at[place].set(jnp.concatenate([small_term, large_term], 0))
    reduced = lax.psum_scatter(slots, "fsdp", scatter_dimension=0, tiled=True).astype(jnp.float32)
    grad_full = lax.psum(reduced.astype(jnp.bfloat16), "dp").astype(jnp.float32)
    new_master, new_moment, new_second = adam_update(grad_full, master, moment, second)
    return (input_grad, new_master, new_moment, new_second)


def solution(mesh):
    placed = (
        P(("dp", "fsdp"), None, None, None),
        P(("dp", "fsdp"), None, None, None),
        P("fsdp", None),
        P("fsdp", None),
        P("fsdp", None),
        P(),
        P(),
    )
    return jax.shard_map(
        per_device,
        mesh=mesh,
        in_specs=placed,
        out_specs=(
            P(("dp", "fsdp"), None, None, None),
            P("fsdp", None),
            P("fsdp", None),
            P("fsdp", None),
        ),
        check_vma=False,
    )
```

profile of v0, /device:TPU:0, one launch (start us, length us, event | category | flops | bytes accessed | tf_op | source)
XLA Modules:
  0.0 905.6 jit_solution(10587041998315581894)
XLA Ops:
  7.2 2.1 fusion.34
  9.4 3.8 fusion.35
  17.0 100.5 %all-gather.3.cloned.1.call-done = bf16[32,1748,128]{2,1,0:T(8,128)(2,1)} async-done(((bf16[1,1748,128]{2,1,0:T(8,128)(2,1)}), bf16[32,1748,128]{2,1,0:T(8,128)(2,1)}) %all-gather.3.cloned.1.call-update) | async-done | bytes 14319632 | tf_op jit(solution)/shard_map/all_gather | solution.py:157
  117.4 17.0 %reshape.222 = bf16[55936,128]{1,0:T(8,128)(2,1)} reshape(bf16[32,1748,128]{2,1,0:T(8,128)(2,1)} %all-gather.3.cloned.1.call-done) | data formatting | bytes 28639232
  134.4 75.8 %gather_fusion = bf16[37212,128]{1,0:T(8,128)(2,1)} fusion(bf16[55936,128]{1,0:T(8,128)(2,1)} %reshape.222, s32[37888]{0:T(1024)S(1)} %pad_clamp_fusion), kind=kCustom, calls=%fused_computation | custom fusion | bytes 19201392 | tf_op jit(solution)/shard_map/jit(_take)/gather | solution.py:159
  210.2 20.6 %broadcast_select_fusion = bf16[37212,128]{1,0:T(8,128)(2,1)S(1)} fusion(bf16[37212,128]{1,0:T(8,128)(2,1)} %gather_fusion, pred[37212]{0:T(1024)(128)(4,1)S(1)} %get-tuple-element.24), kind=kLoop, calls=%fused_computation.6 | loop fusion | flops 4763136 | bytes 19089756 | tf_op jit(solution)/shard_map/jit(_take)/select_n | solution.py:159
  230.9 3.8 fusion.50
  234.7 8.2 reshape.192
  242.9 8.3 reshape.223
  251.9 15.6 %fusion.51 = (f32[22,22,768]{2,1,0:T(8,128)}, f32[1,22,22,768]{3,0,2,1:T(1,128)S(1)}) fusion(bf16[7,7,1,768]{3,2,1,0:T(2,128)(2,1)} %reshape.224, bf16[1,28,22,768]{3,2,1,0:T(8,128)(2,1)S(1)} %maximum_bitcast_fusion), kind=kOutput, calls=%fused_computation.95 | convolution fusion | flops 33589248 | bytes 3995136 | tf_op jit(solution)/shard_map/jvp()/conv_general_dilated | solution.py:50
  268.3 5.9 convert_reduce_fusion
  275.3 5.0 convert_reduce_fusion.1
  281.4 9.3 %reshape.190 = bf16[3072,768]{1,0:T(8,128)(2,1)} reshape(bf16[18432,128]{1,0:T(8,128)(2,1)} %get-tuple-element.31) | data formatting | bytes 9437184 | tf_op jit(solution)/shard_map/reshape | solution.py:39
  290.7 6.0 multiply_convert_fusion
  296.7 5.3 fusion.52
  302.0 5.9 dot_general.22
  307.9 6.2 multiply_reduce_fusion.1
  316.9 53.8 %fusion.23 = bf16[7,7,768]{2,1,0:T(8,128)(2,1)S(1)} fusion(bf16[1,28,22,768]{3,2,1,0:T(8,128)(2,1)S(1)} %copy-done.9, f32[1,22,22,768]{3,2,1,0:T(8,128)S(1)} %get-tuple-element.33), kind=kOutput, calls=%fused_computation.47 | convolution fusion | flops 201573120 | bytes 2508288 | tf_op jit(solution)/shard_map/transpose(jvp())/conv_general_dilated | solution.py:50
  370.8 7.1 convolution_convert_fusion
  377.9 5.0 multiply_reduce_fusion.3
  384.3 5.2 fusion.11
  389.5 1.4 copy.36
  390.9 2.5 constant_dynamic-update-slice_fusion.2
  393.4 9.2 %convert_element_type.175 = bf16[2359296]{0:T(1024)(128)(2,1)} reshape(bf16[3072,768]{1,0:T(8,128)(2,1)} %convolution_convert_fusion) | data formatting | bytes 9437184 | tf_op jit(solution)/shard_map/convert_element_type | solution.py:131
  403.2 5.4 constant_dynamic-update-slice_fusion
  408.7 1.4 dynamic-update-slice.3
  410.1 1.4 dynamic-update-slice.4
  411.5 155.5 %scatter_custom_fusion = bf16[55936,128]{1,0:T(8,128)(2,1)} fusion(s32[37212]{0:T(1024)} %compare_select_fusion, bf16[36900,128]{1,0:T(8,128)(2,1)} %bitcast.76, bf16[]{:T(256)} %constant.114, bf16[312,128]{1,0:T(8,128)(2,1)S(1)} %maximum_bitcast_fusion.1, bf16[]{:T(256)} %constant.82.clone.1), kind=kCustom, calls=%fused_computation.2 | custom fusion | flops 19052544 | bytes 23847936 | tf_op jit(solution)/shard_map/scatter | solution.py:168
  568.1 297.5 %reduce-scatter.5.cloned.1.call-done = bf16[3496,128]{1,0:T(8,128)(2,1)} async-done(((bf16[55936,128]{1,0:T(8,128)(2,1)}), bf16[3496,128]{1,0:T(8,128)(2,1)}) %reduce-scatter.5.cloned.1.call-update) | async-done | bytes 894992
  865.6 10.5 %add_convert_fusion.1 = bf16[1,22,22,768]{3,0,2,1:T(2,128)(2,1)S(1)} fusion(bf16[7,7,768,1]{2,3,1,0:T(2,128)(2,1)S(1)} %reshape.226, f32[1,22,22,768]{3,2,1,0:T(8,128)S(1)} %copy-done.4, bf16[1,22,22,768]{3,2,1,0:T(8,128)(2,1)S(1)} %copy-done.1), kind=kOutput, calls=%fused_computation.38 | convolution fusion | flops 186946560 | bytes 3048960 | tf_op jit(solution)/shard_map/slice | solution.py:165
  877.1 16.0 %all-reduce.3.cloned.1.call-done = bf16[3496,128]{1,0:T(8,128)(2,1)} async-done(((bf16[3496,128]{1,0:T(8,128)(2,1)}), bf16[3496,128]{1,0:T(8,128)(2,1)}) %all-reduce.3.cloned.1.call-update) | async-done | bytes 894992 | tf_op jit(solution)/shard_map/psum | solution.py:170
  893.1 5.5 multiply_subtract_fusion
  (68 shorter events, 14.4 us)
Async XLA Ops:
  7.2 2.2 copy-start.1
  7.2 110.2 %all-gather.3.cloned.1.call-start = ((), (), s32[]{:S(2)}) async-start(), calls=%async_computation.2 | async-start | bytes 14800896 | tf_op jit(solution)/shard_map/all_gather | solution.py:157
  9.4 856.2 %reduce-scatter.5.cloned.1.call-start = ((), (), s32[]{:S(2)}) async-start(), calls=%async_computation.3 | async-start | bytes 15214592
  14.5 1.4 copy-start.14
  14.5 1.4 copy-start.15
  15.9 236.0 %copy-start.8 = (bf16[1,28,22,768]{3,2,1,0:T(8,128)(2,1)}, bf16[1,28,22,768]{3,2,1,0:T(8,128)(2,1)S(1)}, u32[]{:S(2)}) copy-start(bf16[1,28,22,768]{3,2,1,0:T(8,128)(2,1)S(1)} %maximum_bitcast_fusion) | copy-start | bytes 2838532
  230.9 20.2 %copy-start.12 = (bf16[294,128]{1,0:T(8,128)(2,1)}, bf16[294,128]{1,0:T(8,128)(2,1)S(1)}, u32[]{:S(2)}) copy-start(bf16[294,128]{1,0:T(8,128)(2,1)S(1)} %slice.57) | copy-start | bytes 225796
  281.4 9.3 %copy-start.10 = (bf16[484,768]{1,0:T(8,128)(2,1)S(1)}, bf16[484,768]{1,0:T(8,128)(2,1)}, u32[]{:S(2)}) copy-start(bf16[484,768]{1,0:T(8,128)(2,1)} %convert_element_type.157) | copy-start | bytes 2230276
  290.7 6.0 copy-start
  290.7 6.0 copy-start.11
  314.9 2.0 copy-start.9
  315.7 1.2 copy-start.3
  316.9 53.9 %copy-start.6 = (f32[484,768]{1,0:T(8,128)S(1)}, f32[484,768]{1,0:T(8,128)}, u32[]{:S(2)}) copy-start(f32[484,768]{1,0:T(8,128)} %reshape.201) | copy-start | bytes 4460548
  370.8 7.1 copy-start.7
  370.8 7.1 copy-start.16
  377.9 5.0 copy-start.5
  567.1 0.9 copy-start.13
  567.1 298.5 %copy-start.4 = (f32[1,22,22,768]{3,2,1,0:T(8,128)S(1)}, f32[1,22,22,768]{3,2,1,0:T(8,128)}, u32[]{:S(2)}) copy-start(f32[1,22,22,768]{3,2,1,0:T(8,128)} %copy-done.3) | copy-start | bytes 4460548
  567.1 326.0 %all-reduce.3.cloned.1.call-start = ((), (), s32[]{:S(2)}) async-start(), calls=%async_computation.1 | async-start | bytes 1789952 | tf_op jit(solution)/shard_map/psum | solution.py:170
  876.1 17.0 %copy-start.2 = (f32[3496,128]{1,0:T(8,128)S(1)}, f32[3496,128]{1,0:T(8,128)}, u32[]{:S(2)}) copy-start(f32[3496,128]{1,0:T(8,128)} %param.9) | copy-start | bytes 5369860
Sparse Core Ops, SparseCore 0:
  11.4 105.9 all-gather.2
  567.2 298.3 reduce-scatter.4
  867.9 25.1 all-reduce.2
where the time goes:
time: 911 us; the launch traced here: 906 us
  waiting for transfers between devices  414 us (45%)
  other arithmetic  201 us (22%)
  local copies, waits for them, and re-layouts  161 us (18%)
  matrix products  115 us (13%)
  between operations  14.5 us (2%)
    unnamed x4, waiting for transfers between devices  298 us
    scatter x1, other arithmetic, per_device(): slots = slots.at[place].set(jnp.concatenate([small_term, large_term], 0))  156 us
    all_gather x1, waiting for transfers between devices, per_device(): gathered = lax.all_gather(mine, ('dp', 'fsdp'), axis=0, tiled=True)  100 us
    gather x1, local copies, waits for them, and re-layouts, per_device(): flat = jnp.take(gathered, lookup, axis=0)  75.8 us
    conv_general_dilated x2, matrix products, conv_norm(): lax.conv_general_dilated(window[None], kernel, (1, 1), ((0, 0), (reach, r...  69.4 us
    unnamed x42, local copies, waits for them, and re-layouts  33.5 us
    reshape x3, local copies, waits for them, and re-layouts, split_params(): pieces.append(values[start:start + count].reshape(shape))  25.7 us
    select_n x1, other arithmetic, per_device(): flat = jnp.take(gathered, lookup, axis=0)  20.6 us
  transfers between devices with their start and end apart: 3, of which 3 were waited for; matrix products, arithmetic and copies ran while one was open for 2% of the time, Pallas kernels for 0%

commit v1 on v0

v1 whole, which is shorter than its diff:
```python
import functools

import jax
import jax.numpy as jnp
from jax import lax
from jax.experimental import pallas as pl
from jax.experimental.pallas import tpu as pltpu
from jax.sharding import PartitionSpec as P

C = 768
FF = 3072
KSIZE = 7
TAPS = KSIZE * KSIZE
REACH = KSIZE // 2
SIDE = 22
WIDE = 24

LANES = 128
C_ROWS = C // LANES
FF_ROWS = FF // LANES
HEAD = TAPS + 3
IN_AT = HEAD * C_ROWS
BIN_AT = IN_AT + C * FF_ROWS
OUT_AT = BIN_AT + FF_ROWS
TAIL_AT = OUT_AT + FF * C_ROWS
P_ROWS = TAIL_AT + 2 * C_ROWS
SMALL = 64
STEPS = 6
IN_COLS = FF // STEPS
OUT_ROWS = FF // STEPS
CHUNK = 160
MARGIN = 4096

ROOT_HALF = 0.7071067811865476
DENSITY = 0.3989422804014327
LEARNING = 0.001
DECAY = 0.05
BETA_ONE = 0.9
BETA_TWO = 0.95
FIRST_FIX = 0.9999734386011124
SECOND_FIX = 0.994079470779666

F32 = jnp.float32
BF16 = jnp.bfloat16


def shift_copies(source, padded, shifts, lanes):
    padded[REACH : REACH + SIDE, 8 : 8 + WIDE, :] = source[:, :, lanes].astype(F32)
    for b in range(KSIZE):
        shifts[b] = padded[:, 8 - REACH + b : 8 - REACH + b + WIDE, :]


def lane_block(block):
    return pl.ds(pl.multiple_of(block * LANES, LANES), LANES)


def mix_body(image, small, normed, scaled, inverse, padded, shifts, mixed):
    padded[...] = jnp.zeros_like(padded)

    def channels(block, carry):
        lanes = lane_block(block)
        shift_copies(image, padded, shifts, lanes)

        def rows(group, carry):
            at = group * 11
            total = jnp.broadcast_to(small[TAPS : TAPS + 1, lanes][None], (11, WIDE, LANES))
            for a in range(KSIZE):
                for b in range(KSIZE):
                    tap = small[a * KSIZE + b : a * KSIZE + b + 1, lanes]
                    total = total + tap[None] * shifts[b, pl.ds(at + a, 11)]
            mixed[pl.ds(at, 11), :, lanes] = total
            return carry

        return lax.fori_loop(0, SIDE // 11, rows, carry)

    lax.fori_loop(0, C_ROWS, channels, 0)

    def norm(row, carry):
        value = mixed[row]
        centred = value - jnp.mean(value, -1, keepdims=True)
        spread = jnp.mean(centred * centred, -1, keepdims=True)
        inv = lax.rsqrt(spread + 1e-06)
        unit = centred * inv
        scaled[row] = unit
        inverse[row] = jnp.broadcast_to(inv, (WIDE, LANES))
        normed[row] = (unit * small[TAPS + 1 : TAPS + 2, :] + small[TAPS + 2 : TAPS + 3, :]).astype(BF16)
        return carry

    lax.fori_loop(0, SIDE, norm, 0)


def mix(image, small):
    return pl.pallas_call(
        mix_body,
        out_shape=[
            jax.ShapeDtypeStruct((SIDE, WIDE, C), BF16),
            jax.ShapeDtypeStruct((SIDE, WIDE, C), F32),
            jax.ShapeDtypeStruct((SIDE, WIDE, LANES), F32),
        ],
        scratch_shapes=[
            pltpu.VMEM((SIDE + 2 * REACH, 40, LANES), F32),
            pltpu.VMEM((KSIZE, SIDE + 2 * REACH, WIDE, LANES), F32),
            pltpu.VMEM((SIDE, WIDE, C), F32),
        ],
        name="mix",
    )(image, small)


def unmix_body(
    image, cotangent, small, upstream, scaled, inverse, result, grads, padded, shifts, mixed_grad, taps
):
    padded[...] = jnp.zeros_like(padded)
    grads[...] = jnp.zeros_like(grads)
    gain = small[TAPS + 1 : TAPS + 2, :]

    def fold(value):
        return value[0:8] + value[8:16] + value[16:24]

    def norm(row, carry):
        bias_sum, gain_sum, shift_sum = carry
        up = upstream[row]
        unit = scaled[row]
        inv = inverse[row][:, 0:1]
        scaled_up = up * gain
        first = jnp.mean(scaled_up, -1, keepdims=True)
        second = jnp.mean(scaled_up * unit, -1, keepdims=True)
        value = inv * (scaled_up - first - unit * second)
        mixed_grad[row] = value
        return bias_sum + fold(value), gain_sum + fold(up * unit), shift_sum + fold(up)

    zero = jnp.zeros((8, C), F32)
    sums = lax.fori_loop(0, SIDE, norm, (zero, zero, zero))
    for k in range(3):
        grads[TAPS + k : TAPS + k + 1, :] = jnp.sum(sums[k], 0, keepdims=True)

    def channels(block, carry):
        lanes = lane_block(block)
        shift_copies(mixed_grad, padded, shifts, lanes)
        taps[...] = jnp.zeros_like(taps)

        def rows(group, carry):
            at = group * 2
            source = image[pl.ds(at, 2), :, lanes].astype(F32)
            total = jnp.zeros((2, WIDE, LANES), F32)
            for a in range(KSIZE):
                for b in range(KSIZE):
                    index = TAPS - 1 - (a * KSIZE + b)
                    piece = shifts[b, pl.ds(at + a, 2)]
                    total = total + small[index : index + 1, lanes][None] * piece
                    product = source * piece
                    taps[index] += fold(product[0] + product[1])
            out = cotangent[pl.ds(at, 2), :, lanes].astype(F32) + total
            result[pl.ds(at, 2), :, lanes] = out.astype(BF16)
            return carry

        lax.fori_loop(0, SIDE // 2, rows, 0)
        for index in range(TAPS):
            grads[index : index + 1, lanes] = jnp.sum(taps[index], 0, keepdims=True)
        return carry

    lax.fori_loop(0, C_ROWS, channels, 0)


def unmix(image, cotangent, small, upstream, scaled, inverse):
    return pl.pallas_call(
        unmix_body,
        out_shape=[
            jax.ShapeDtypeStruct((SIDE, WIDE, C), BF16),
            jax.ShapeDtypeStruct((SMALL, C), F32),
        ],
        scratch_shapes=[
            pltpu.VMEM((SIDE + 2 * REACH, 40, LANES), F32),
            pltpu.VMEM((KSIZE, SIDE + 2 * REACH, WIDE, LANES), F32),
            pltpu.VMEM((SIDE, WIDE, C), F32),
            pltpu.VMEM((TAPS, 8, LANES), F32),
        ],
        name="unmix",
    )(image, cotangent, small, upstream, scaled, inverse)


def unpack_body(parts, rows, owners, order, starts, counts, slots, small, w_in, w_out, flat):
    step = pl.program_id(0)

    @pl.when(step < owners)
    def _():
        start = starts[step]
        count = counts[step]
        for part in range(parts):
            left = jnp.clip(count - part * rows, 0, rows)
            trips = (left + CHUNK - 1) // CHUNK

            def copy(k, carry, part=part):
                at = pl.multiple_of(k * CHUNK, 16)
                piece = slots[part, pl.ds(at, CHUNK), :].astype(F32)
                flat[pl.ds(start + part * rows + k * CHUNK, CHUNK), :] = piece
                return carry

            lax.fori_loop(0, trips, copy, 0)

    @pl.when(step == owners)
    def _():
        for j in range(C_ROWS):
            lane = slice(j * LANES, (j + 1) * LANES)
            small[0:HEAD, lane] = flat[pl.ds(j, HEAD, stride=C_ROWS), :]
            small[HEAD : HEAD + 4, lane] = flat[pl.ds(BIN_AT + j, 4, stride=C_ROWS), :]
            small[HEAD + 4 : HEAD + 6, lane] = flat[pl.ds(TAIL_AT + j, 2, stride=C_ROWS), :]

    @pl.when(step >= owners)
    def _():
        block = step - owners
        for j in range(IN_COLS // LANES):
            at = IN_AT + block * (IN_COLS // LANES) + j
            w_in[:, j * LANES : (j + 1) * LANES] = flat[pl.ds(at, C, stride=FF_ROWS), :].astype(BF16)
        for j in range(C_ROWS):
            at = OUT_AT + block * (OUT_ROWS * C_ROWS) + j
            w_out[:, j * LANES : (j + 1) * LANES] = flat[pl.ds(at, OUT_ROWS, stride=C_ROWS), :].astype(BF16)


def unpack(gathered, order, starts, counts):
    parts, span, _ = gathered.shape
    owners = order.shape[0]
    rows = span // owners
    late = lambda i: jnp.maximum(i - owners, 0)
    grid_spec = pltpu.PrefetchScalarGridSpec(
        num_scalar_prefetch=3,
        grid=(owners + STEPS,),
        in_specs=[
            pl.BlockSpec(
                (parts, rows, LANES),
                lambda i, o, s, c: (0, o[jnp.minimum(i, owners - 1)], 0),
            )
        ],
        out_specs=[
            pl.BlockSpec((SMALL, C), lambda i, o, s, c: (0, 0)),
            pl.BlockSpec((C, IN_COLS), lambda i, o, s, c: (0, late(i))),
            pl.BlockSpec((OUT_ROWS, C), lambda i, o, s, c: (late(i), 0)),
        ],
        scratch_shapes=[pltpu.VMEM((P_ROWS + MARGIN, LANES), F32)],
    )
    return pl.pallas_call(
        functools.partial(unpack_body, parts, rows, owners),
        grid_spec=grid_spec,
        out_shape=[
            jax.ShapeDtypeStruct((SMALL, C), F32),
            jax.ShapeDtypeStruct((C, FF), BF16),
            jax.ShapeDtypeStruct((FF, C), BF16),
        ],
        name="unpack",
    )(order, starts, counts, gathered)


def pack_body(paired, groups, owners, bases, *refs):
    inputs = 5 if paired else 3
    small = refs[0]
    in_refs = refs[1:inputs:2] if paired else refs[1:2]
    out_refs = refs[2:inputs:2] if paired else refs[2:3]
    outs = refs[inputs:-1]
    flat = refs[-1]
    step = pl.program_id(0)

    def total(parts, index):
        value = parts[0][index].astype(F32)
        for other in parts[1:]:
            value = value + other[index].astype(F32)
        return value

    @pl.when(step == 0)
    def _():
        for j in range(C_ROWS):
            lane = slice(j * LANES, (j + 1) * LANES)
            flat[pl.ds(j, HEAD, stride=C_ROWS), :] = small[0:HEAD, lane]
            flat[pl.ds(BIN_AT + j, 4, stride=C_ROWS), :] = small[HEAD : HEAD + 4, lane]
            flat[pl.ds(TAIL_AT + j, 2, stride=C_ROWS), :] = small[HEAD + 4 : HEAD + 6, lane]
        flat[P_ROWS : P_ROWS + MARGIN, :] = jnp.zeros((MARGIN, LANES), F32)

    @pl.when(step < STEPS)
    def _():
        for j in range(IN_COLS // LANES):
            at = IN_AT + step * (IN_COLS // LANES) + j
            index = (slice(None), slice(j * LANES, (j + 1) * LANES))
            flat[pl.ds(at, C, stride=FF_ROWS), :] = total(in_refs, index)
        for j in range(C_ROWS):
            at = OUT_AT + step * (OUT_ROWS * C_ROWS) + j
            index = (slice(None), slice(j * LANES, (j + 1) * LANES))
            flat[pl.ds(at, OUT_ROWS, stride=C_ROWS), :] = total(out_refs, index)

    slot = step - STEPS
    for (table, first, count, row, rows), out in zip(groups, outs, strict=True):

        @pl.when((slot >= first) & (slot < first + count))
        def _(table=table, row=row, rows=rows, out=out):
            base = bases[table * owners + slot] + row
            for at in range(0, rows, 16):
                out[0, at : at + 16, :] = flat[pl.ds(base + at, 16), :].astype(BF16)


def pack(bases, small, ins, outs, owners, groups):
    paired = len(ins) == 2
    early = lambda i: jnp.minimum(i, STEPS - 1)
    operands = [small]
    in_specs = [pl.BlockSpec((SMALL, C), lambda i, b: (0, 0))]
    for w_in, w_out in zip(ins, outs, strict=True):
        operands += [w_in, w_out]
        in_specs += [
            pl.BlockSpec((C, IN_COLS), lambda i, b: (0, early(i))),
            pl.BlockSpec((OUT_ROWS, C), lambda i, b: (early(i), 0)),
        ]
    out_specs = [
        pl.BlockSpec(
            (1, rows, LANES),
            lambda i, b, first=first, count=count: (jnp.clip(i - STEPS - first, 0, count - 1), 0, 0),
        )
        for table, first, count, row, rows in groups
    ]
    grid_spec = pltpu.PrefetchScalarGridSpec(
        num_scalar_prefetch=1,
        grid=(STEPS + owners,),
        in_specs=in_specs,
        out_specs=out_specs,
        scratch_shapes=[pltpu.VMEM((P_ROWS + MARGIN, LANES), F32)],
    )
    return pl.pallas_call(
        functools.partial(pack_body, paired, groups, owners),
        grid_spec=grid_spec,
        out_shape=[
            jax.ShapeDtypeStruct((count, rows, LANES), BF16) for table, first, count, row, rows in groups
        ],
        name="pack",
    )(bases, *operands)


def add(*values):
    total = values[0].astype(F32)
    for value in values[1:]:
        total = total + value.astype(F32)
    return total


def swap(value, mask, size):
    return lax.ppermute(value, "fsdp", [(i, i ^ mask) for i in range(size)])


def reduce_part(far, near, home, masks, size):
    got = swap(far, masks[0], size)
    half = near.shape[0]
    near = add(near, got[half:]).astype(BF16)
    back = swap(near, masks[1], size)
    home = add(home, got[:half], back)
    low = home.astype(BF16)
    pieces = [swap(low[k], 4 * k, size) for k in (1, 2, 3)]
    return add(home[0], *pieces).astype(BF16)


def image_pass(image, cot_image, small, weight_in, weight_out):
    bias_in = small[HEAD : HEAD + 4].reshape(-1)
    bias_out, layer_scale = small[HEAD + 4], small[HEAD + 5]
    normed, scaled, inverse = mix(image, small)
    normed_low = normed.reshape(-1, C)
    before = jnp.dot(normed_low, weight_in, preferred_element_type=F32) + bias_in
    activated = (before * 0.5 * (1.0 + lax.erf(before * ROOT_HALF))).astype(BF16)
    branch = jnp.dot(activated, weight_out, preferred_element_type=F32) + bias_out
    cot_flat = cot_image.reshape(-1, C).astype(F32)
    branch_grad = (layer_scale * cot_flat).astype(BF16)
    grad_scale = jnp.sum(cot_flat * branch, 0)
    grad_bias_out = jnp.sum(branch_grad.astype(F32), 0)
    grad_weight_out = lax.dot_general(
        activated, branch_grad, (((0,), (0,)), ((), ())), preferred_element_type=F32
    ).astype(BF16)
    activated_grad = lax.dot_general(
        branch_grad, weight_out, (((1,), (1,)), ((), ())), preferred_element_type=F32
    )
    slope = (
        0.5 * (1.0 + lax.erf(before * ROOT_HALF))
        + before * jnp.exp(-0.5 * before * before) * DENSITY
    )
    before_grad = (activated_grad * slope).astype(BF16)
    grad_bias_in = jnp.sum(before_grad.astype(F32), 0)
    grad_weight_in = lax.dot_general(
        normed_low, before_grad, (((0,), (0,)), ((), ())), preferred_element_type=F32
    ).astype(BF16)
    normed_grad = lax.dot_general(
        before_grad, weight_in, (((1,), (1,)), ((), ())), preferred_element_type=F32
    )
    result, head_grad = unmix(
        image, cot_image, small, normed_grad.reshape(SIDE, WIDE, C), scaled, inverse
    )
    small_grad = jnp.concatenate(
        [
            head_grad[:HEAD],
            grad_bias_in.reshape(-1, C),
            grad_bias_out[None],
            grad_scale[None],
            jnp.zeros((SMALL - HEAD - 6, C), F32),
        ]
    ).astype(BF16)
    return small_grad, grad_weight_in, grad_weight_out, result


def adam_update(gradient, weights, first, second_moment):
    first_new = BETA_ONE * first + (1.0 - BETA_ONE) * gradient
    second_new = BETA_TWO * second_moment + (1.0 - BETA_TWO) * gradient * gradient
    update = first_new / FIRST_FIX / (jnp.sqrt(second_new / SECOND_FIX) + 1e-08)
    weights_new = weights * (1.0 - LEARNING * DECAY) - LEARNING * update
    return (weights_new, first_new, second_new)


def per_device(images_in, cotangent, master, moment, second, owner, offset):
    owners = lax.axis_size("fsdp")
    replicas = lax.axis_size("dp")
    me = lax.axis_index("fsdp")
    core = lax.axis_index("dp")
    bucket = master.shape[0]
    total_rows = owner.shape[0]
    rows = -(-bucket // (replicas * CHUNK)) * CHUNK

    ids = jnp.arange(owners, dtype=jnp.int32)
    positions = jnp.arange(total_rows, dtype=jnp.int32)
    begins = jnp.where(offset == 0, positions, 0)
    starts = jnp.sum(jnp.where(owner[None, :] == ids[:, None], begins[None, :], 0), 1)
    rank = jnp.sum((starts[None, :] < starts[:, None]).astype(jnp.int32), 1)
    later = jnp.where(starts[None, :] > starts[:, None], starts[None, :], total_rows)
    counts = jnp.min(later, 1) - starts
    chosen = rank[None, :] == ids[:, None]
    pick = lambda mask, values: jnp.sum(jnp.where(mask, values[None, :], 0), 1)

    lowered = jnp.pad(master, ((0, replicas * rows - bucket), (0, 0))).astype(BF16)
    mine = lax.dynamic_slice_in_dim(lowered, core * rows, rows, 0)
    gathered = lax.all_gather(mine, ("dp", "fsdp"), axis=0, tiled=True)
    small, weight_in, weight_out = unpack(
        gathered.reshape(replicas, owners * rows, LANES),
        pick(chosen, ids),
        pick(chosen, starts),
        pick(chosen, counts),
    )

    widen = lambda value: jnp.pad(value[0], ((0, 0), (0, WIDE - SIDE), (0, 0)))
    small_grad, grad_in, grad_out, result = image_pass(
        widen(images_in), widen(cotangent), small, weight_in, weight_out
    )
    input_grad = result[None, :, :SIDE]

    if replicas == 2 and owners == 16:
        other = lambda value: lax.ppermute(value, "dp", [(0, 1), (1, 0)])
        far_out, far_in, far_small = other(grad_out), other(grad_in), other(small_grad)
        quarter = rows // 32 * 8 // 16 * 16
        sizes = [quarter, quarter, rows // 2 - quarter, rows // 2 - quarter]
        groups = []
        at = 0
        for number, size in enumerate(sizes):
            groups += [(number % 2, f, c, at, size) for f, c in ((8, 8), (4, 4), (0, 4))]
            at += size
        spots = jnp.arange(16, dtype=jnp.int32)
        high, low, deep = spots >> 3, (spots >> 2) & 1, spots & 3
        tables = [deep * 4 + high * 2 + low, deep * 4 + low * 2 + high]
        bases = jnp.concatenate(
            [pick((table ^ me)[:, None] == ids[None, :], starts) for table in tables]
        ) + core * rows
        packed = pack(
            bases, add(small_grad, far_small), (grad_in, far_in), (grad_out, far_out), owners, groups
        )
        sums = [
            reduce_part(*packed[3 * k : 3 * k + 3], (2, 1) if k % 2 == 0 else (1, 2), owners)
            for k in range(4)
        ]
        half = jnp.concatenate(sums, 0)
        theirs = other(half)
        grad_low = jnp.where(
            core == 0, jnp.concatenate([half, theirs]), jnp.concatenate([theirs, half])
        )
    else:
        groups = [(0, 0, owners, part * rows, rows) for part in range(replicas)]
        packed = pack(starts, small_grad.astype(F32), (grad_in,), (grad_out,), owners, groups)
        stacked = jnp.concatenate([value.reshape(owners * rows, LANES) for value in packed])
        part = lax.psum_scatter(stacked, "dp", scatter_dimension=0, tiled=True)
        half = lax.psum_scatter(part, "fsdp", scatter_dimension=0, tiled=True)
        grad_low = lax.all_gather(half, "dp", axis=0, tiled=True)

    mine_count = jnp.sum(jnp.where(ids == me, counts, 0))
    valid = jnp.arange(bucket)[:, None] < mine_count
    grad_full = jnp.where(valid, grad_low[:bucket].astype(F32), 0.0)
    new_master, new_moment, new_second = adam_update(grad_full, master, moment, second)
    return (input_grad, new_master, new_moment, new_second)


def solution(mesh):
    placed = (
        P(("dp", "fsdp"), None, None, None),
        P(("dp", "fsdp"), None, None, None),
        P("fsdp", None),
        P("fsdp", None),
        P("fsdp", None),
        P(),
        P(),
    )
    return jax.shard_map(
        per_device,
        mesh=mesh,
        in_specs=placed,
        out_specs=(
            P(("dp", "fsdp"), None, None, None),
            P("fsdp", None),
            P("fsdp", None),
            P("fsdp", None),
        ),
        check_vma=False,
    )
```

time: 911 us -> 337 us (0.37)
  waiting for transfers between devices: 414 us -> 165 us
  other arithmetic: 201 us -> 17.4 us
  local copies, waits for them, and re-layouts: 161 us -> 8.07 us
  matrix products: 115 us -> 31.6 us
  Pallas kernels: 0 us -> 70.2 us
  starting transfers between devices: 0.12 us -> 29.6 us
    unnamed x4 -> x1, waiting for transfers between devices: 298 us -> 0.02 us
    scatter x1 -> x0, other arithmetic: 156 us -> none  [per_device(): slots = slots.at[place].set(jnp.concatenate([small_term, large_term], 0))]
    gather x1 -> x0, local copies, waits for them, and re-layouts: 75.8 us -> none  [per_device(): flat = jnp.take(gathered, lookup, axis=0)]
    pallas_call x0 -> x4, Pallas kernels: none -> 70.2 us  [the longest x1 18.9 us: unmix(): pl.pallas_call(unmix_body, out_shape=[jax.ShapeDtypeStruct((SIDE, WIDE, C...]
    conv_general_dilated x2 -> x0, matrix products: 69.4 us -> none  [conv_norm(): lax.conv_general_dilated(window[None], kernel, (1, 1), ((0, 0), (reach, r...]
    ppermute x0 -> x24, waiting for transfers between devices: none -> 60.7 us  [the longest x20 60.2 us: swap(): return lax.ppermute(value, 'fsdp', [(i, i ^ mask) for i in range(size)])]
    unnamed x42 -> x41, local copies, waits for them, and re-layouts: 33.5 us -> 0.13 us
    ppermute x0 -> x24, starting transfers between devices: none -> 29.6 us  [the longest x20 28.7 us: swap(): return lax.ppermute(value, 'fsdp', [(i, i ^ mask) for i in range(size)])]
  transfers between devices with their start and end apart: 3 -> 25, of which waited for: 3 -> 10; matrix products, arithmetic and copies ran while one was open for 2% -> 7% of each run, Pallas kernels for 0% -> 6%
where the time goes in v1:
time: 337 us; the launch traced here: 336 us
  waiting for transfers between devices  165 us (49%)
  Pallas kernels  70.2 us (21%)
  matrix products  31.6 us (9%)
  starting transfers between devices  29.6 us (9%)
  other arithmetic  17.4 us (5%)
  between operations  14.4 us (4%)
  local copies, waits for them, and re-layouts  8.07 us (2%)
    all_gather x1, waiting for transfers between devices, per_device(): gathered = lax.all_gather(mine, ('dp', 'fsdp'), axis=0, tiled=True)  104 us
    ppermute x20, waiting for transfers between devices, swap(): return lax.ppermute(value, 'fsdp', [(i, i ^ mask) for i in range(size)])  60.2 us
    ppermute x20, starting transfers between devices, swap(): return lax.ppermute(value, 'fsdp', [(i, i ^ mask) for i in range(size)])  28.7 us
    pallas_call x1, Pallas kernels, unmix(): pl.pallas_call(unmix_body, out_shape=[jax.ShapeDtypeStruct((SIDE, WIDE, C...  18.9 us
    pallas_call x1, Pallas kernels, unpack(): pl.pallas_call(functools.partial(unpack_body, parts, rows, owners), grid_...  18.6 us
    pallas_call x1, Pallas kernels, pack(): pl.pallas_call(functools.partial(pack_body, paired, groups, owners), grid...  18.1 us
    pallas_call x1, Pallas kernels, mix(): pl.pallas_call(mix_body, out_shape=[jax.ShapeDtypeStruct((SIDE, WIDE, C),...  14.7 us
  transfers between devices with their start and end apart: 25, of which 10 were waited for; matrix products, arithmetic and copies ran while one was open for 7% of the time, Pallas kernels for 6%

profile of v1, /device:TPU:0, one launch (start us, length us, event | category | flops | bytes accessed | tf_op | source)
XLA Modules:
  0.0 336.3 jit_solution(17494916530718808489)
XLA Ops:
  7.2 1.7 convert.23
  13.6 104.2 %all-gather.2.cloned.1.call-done = bf16[56320,128]{1,0:T(8,128)(2,1)} async-done(((bf16[1760,128]{1,0:T(8,128)(2,1)}), bf16[56320,128]{1,0:T(8,128)(2,1)}) %all-gather.2.cloned.1.call-update) | async-done | bytes 14417936 | tf_op jit(solution)/shard_map/all_gather | solution.py:428
  117.8 18.6 %unpack.1 = (f32[64,768]{1,0:T(8,128)}, bf16[768,3072]{1,0:T(8,128)(2,1)}, bf16[3072,768]{1,0:T(8,128)(2,1)}) custom-call(s32[16]{0:T(128)} %get-tuple-element.50.order, s32[16]{0:T(128)} %get-tuple-element.49.starts, s32[16]{0:T(128)} %select_reduce_fusion.3.counts, bf16[2,28160,128]{2,1,0:T(8,128)(2,1)} %bitcast.94), custom_call_target="tpu_custom_call" | custom-call | tf_op jit(solution)/shard_map/unpack/pallas_call | solution.py:240
  137.9 14.7 %mix.1 = (bf16[22,24,768]{2,1,0:T(8,128)(2,1)}, f32[22,24,768]{2,1,0:T(8,128)}, f32[22,24,128]{2,1,0:T(8,128)}) custom-call(bf16[22,24,768]{2,1,0:T(8,128)(2,1)} %pad.12.image, f32[64,768]{1,0:T(8,128)} %get-tuple-element.24.small), custom_call_target="tpu_custom_call" | custom-call | tf_op jit(solution)/shard_map/mix/pallas_call | solution.py:93
  152.8 5.8 %multiply_convert_fusion = (bf16[528,3072]{1,0:T(8,128)(2,1)S(1)}, f32[528,3072]{1,0:T(8,128)S(1)}) fusion(f32[3072]{0:T(1024)S(1)} %add.158, bf16[528,768]{1,0:T(8,128)(2,1)} %bitcast.103, bf16[768,3072]{1,0:T(8,128)(2,1)} %get-tuple-element.27), kind=kOutput, calls=%fused_computation.7 | convolution fusion | flops 2501148672 | bytes 15273984 | tf_op jit(solution)/shard_map/dot_general | solution.py:359
  158.6 4.7 %fusion.45 = (bf16[3072]{0:T(1024)(128)(2,1)S(1)}, bf16[528,3072]{1,0:T(8,128)(2,1)S(1)}) fusion(f32[528,3072]{1,0:T(8,128)S(1)} %get-tuple-element.91, f32[3072]{0:T(1024)S(1)} %add.158, bf16[528,768]{1,0:T(8,128)(2,1)S(1)} %fusion.8, bf16[3072,768]{1,0:T(8,128)(2,1)S(1)} %bitcast.100), kind=kOutput, calls=%fused_computation.113 | convolution fusion | flops 2510877696 | bytes 15280128 | tf_op jit(solution)/shard_map/dot_general | solution.py:369
  163.4 5.6 %convolution_convert_fusion.1.refs_1_ = bf16[768,3072]{1,0:T(8,128)(2,1)} fusion(bf16[528,768]{1,0:T(8,128)(2,1)S(1)} %bitcast.104, bf16[528,3072]{1,0:T(8,128)(2,1)S(1)} %get-tuple-element.89), kind=kOutput, calls=%fused_computation.10 | convolution fusion | flops 2493775872 | bytes 8773632 | tf_op jit(solution)/shard_map/dot_general | solution.py:378
  169.0 5.6 %convolution_convert_fusion.refs_2_ = bf16[3072,768]{1,0:T(8,128)(2,1)} fusion(bf16[528,3072]{1,0:T(8,128)(2,1)S(1)} %get-tuple-element.90, bf16[528,768]{1,0:T(8,128)(2,1)S(1)} %fusion.8), kind=kOutput, calls=%fused_computation.9 | convolution fusion | flops 2493775872 | bytes 8773632 | tf_op jit(solution)/shard_map/dot_general | solution.py:366
  176.2 3.9 %fusion.46 = f32[528,768]{1,0:T(8,128)} fusion(bf16[528,3072]{1,0:T(8,128)(2,1)S(1)} %get-tuple-element.89, bf16[768,3072]{1,0:T(8,128)(2,1)S(1)} %bitcast.102), kind=kOutput, calls=%fused_computation.114 | convolution fusion | flops 2491416576 | bytes 9584640 | tf_op jit(solution)/shard_map/dot_general | solution.py:381
  180.1 18.9 %unmix.1 = (bf16[22,24,768]{2,1,0:T(8,128)(2,1)}, f32[64,768]{1,0:T(8,128)}) custom-call(bf16[22,24,768]{2,1,0:T(8,128)(2,1)} %pad.12.image, bf16[22,24,768]{2,1,0:T(8,128)(2,1)} %get-tuple-element.73.cotangent, f32[64,768]{1,0:T(8,128)} %get-tuple-element.24.small, f32[22,24,768]{2,1,0:T(8,128)} %bitcast.97, f32[22,24,768]{2,1,0:T(8,128)} %get-tuple-element.28.scaled, ...), custom_call_target="tpu_custom_call" | custom-call | tf_op jit(solution)/shard_map/unmix/pallas_call | solution.py:165
  200.0 6.0 %fusion.9 = bf16[768]{0:T(1024)(128)(2,1)S(1)} fusion(bf16[22,24,768]{2,1,0:T(8,128)(2,1)S(1)} %copy-done.2, bf16[528,3072]{1,0:T(8,128)(2,1)} %copy-done.14, bf16[3072,768]{1,0:T(8,128)(2,1)} %get-tuple-element.25, f32[768]{0:T(1024)S(1)} %get-tuple-element.44), kind=kOutput, calls=%fused_computation.23 | convolution fusion | flops 2493037824 | bytes 8778240 | tf_op jit(solution)/shard_map/dot_general | solution.py:361
  208.2 18.1 %pack.1 = (bf16[8,432,128]{2,1,0:T(8,128)(2,1)}, bf16[4,432,128]{2,1,0:T(8,128)(2,1)}, bf16[4,432,128]{2,1,0:T(8,128)(2,1)}, bf16[8,432,128]{2,1,0:T(8,128)(2,1)...) custom-call(s32[32]{0:T(128)} %add_add_fusion.bases, ...), custom_call_target="tpu_custom_call" | custom-call | tf_op jit(solution)/shard_map/pack/pallas_call | solution.py:322
  226.3 1.5 collective-permute-start.3
  228.4 1.2 collective-permute-start.13
  230.4 18.7 %collective-permute-done.3 = bf16[8,432,128]{2,1,0:T(8,128)(2,1)S(1)} collective-permute-done((bf16[8,432,128]{2,1,0:T(8,128)(2,1)}, bf16[8,432,128]{2,1,0:T(8,128)(2,1)S(1)}, u32[]{:S(2)}, u32[]{:S(2)}) %collective-permute-start.3) | collective-permute-done | bytes 884768 | tf_op jit(solution)/shard_map/ppermute | solution.py:340
  250.2 1.3 collective-permute-start.4
  253.5 15.2 %collective-permute-done.13 = bf16[8,448,128]{2,1,0:T(8,128)(2,1)S(1)} collective-permute-done((bf16[8,448,128]{2,1,0:T(8,128)(2,1)}, bf16[8,448,128]{2,1,0:T(8,128)(2,1)S(1)}, u32[]{:S(2)}, u32[]{:S(2)}) %collective-permute-start.13) | collective-permute-done | bytes 917536 | tf_op jit(solution)/shard_map/ppermute | solution.py:340
  269.9 1.3 collective-permute-start.14
  272.2 7.5 %collective-permute-done.4 = bf16[4,432,128]{2,1,0:T(8,128)(2,1)S(1)} collective-permute-done((bf16[4,432,128]{2,1,0:T(8,128)(2,1)S(1)}, bf16[4,432,128]{2,1,0:T(8,128)(2,1)S(1)}, u32[]{:S(2)}, u32[]{:S(2)}) %collective-permute-start.4) | collective-permute-done | bytes 442400 | tf_op jit(solution)/shard_map/ppermute | solution.py:340
  279.9 1.8 collective-permute-start.7
  282.4 2.0 collective-permute-start.5
  284.6 3.9 %collective-permute-done.14 = bf16[4,448,128]{2,1,0:T(8,128)(2,1)S(1)} collective-permute-done((bf16[4,448,128]{2,1,0:T(8,128)(2,1)S(1)}, bf16[4,448,128]{2,1,0:T(8,128)(2,1)S(1)}, u32[]{:S(2)}, u32[]{:S(2)}) %collective-permute-start.14) | collective-permute-done | bytes 458784 | tf_op jit(solution)/shard_map/ppermute | solution.py:340
  288.5 1.7 collective-permute-start.12
  291.5 2.0 collective-permute-start.10
  293.5 1.7 collective-permute-start.17
  296.3 5.2 %collective-permute-start.15 = (bf16[448,128]{1,0:T(8,128)(2,1)S(1)}, bf16[448,128]{1,0:T(8,128)(2,1)S(1)}, u32[]{:S(2)}, u32[]{:S(2)}) collective-permute-start(bf16[448,128]{1,0:T(8,128)(2,1)S(1)} %get-tuple-element.77), channel_id=1, source_target_pairs={{0,4},{1,5},{2,6},{3,7},{4,0},{5,1},{6,2},{7,3},{8,12},{9,13},{10,... | collective-permute-start | bytes 344072 | tf_op jit(solution)/shard_map/ppermute | solution.py:340
  301.5 6.5 %collective-permute-done.11 = bf16[432,128]{1,0:T(8,128)(2,1)S(1)} collective-permute-done((bf16[432,128]{1,0:T(8,128)(2,1)S(1)}, bf16[432,128]{1,0:T(8,128)(2,1)S(1)}, u32[]{:S(2)}, u32[]{:S(2)}) %collective-permute-start.11) | collective-permute-done | bytes 110624 | tf_op jit(solution)/shard_map/ppermute | solution.py:340
  308.4 4.2 %collective-permute-start.20 = (bf16[448,128]{1,0:T(8,128)(2,1)S(1)}, bf16[448,128]{1,0:T(8,128)(2,1)S(1)}, u32[]{:S(2)}, u32[]{:S(2)}) collective-permute-start(bf16[448,128]{1,0:T(8,128)(2,1)S(1)} %get-tuple-element.74), channel_id=1, source_target_pairs={{0,4},{1,5},{2,6},{3,7},{4,0},{5,1},{6,2},{7,3},{8,12},{9,13},{10,... | collective-permute-start | bytes 344072 | tf_op jit(solution)/shard_map/ppermute | solution.py:340
  312.5 3.7 %collective-permute-done.16 = bf16[448,128]{1,0:T(8,128)(2,1)S(1)} collective-permute-done((bf16[448,128]{1,0:T(8,128)(2,1)S(1)}, bf16[448,128]{1,0:T(8,128)(2,1)S(1)}, u32[]{:S(2)}, u32[]{:S(2)}) %collective-permute-start.16) | collective-permute-done | bytes 114720 | tf_op jit(solution)/shard_map/ppermute | solution.py:340
  316.3 3.7 %collective-permute-done.21 = bf16[448,128]{1,0:T(8,128)(2,1)S(1)} collective-permute-done((bf16[448,128]{1,0:T(8,128)(2,1)S(1)}, bf16[448,128]{1,0:T(8,128)(2,1)S(1)}, u32[]{:S(2)}, u32[]{:S(2)}) %collective-permute-start.21) | collective-permute-done | bytes 114720 | tf_op jit(solution)/shard_map/ppermute | solution.py:340
  321.7 2.3 slice_bitcast_fusion
  325.3 4.1 %multiply_subtract_fusion = (f32[3496,128]{1,0:T(8,128)}, f32[3496,128]{1,0:T(8,128)}, f32[3496,128]{1,0:T(8,128)}) fusion(f32[3496,128]{1,0:T(8,128)S(1)} %copy-done, bf16[3520,128]{1,0:T(8,128)(2,1)S(1)} %constant_dynamic-update-slice_fusion.5, bf16[3520,128]{1,0:T(8,128)(2,1)S(1)} %get-tuple-element.80, pred[]{:T(512)S(6)} %eq.73, ...), kind=kLoop, calls=%fused_computation.15 | loop fusion | flops 7607296 | bytes 12533161 | tf_op jit(solution)/shard_map/sub | solution.py:403
  (117 shorter events, 24.5 us)
Async XLA Ops:
  7.2 110.6 %all-gather.2.cloned.1.call-start = ((), (), s32[]{:S(2)}) async-start(), calls=%async_computation | async-start | bytes 14868480 | tf_op jit(solution)/shard_map/all_gather | solution.py:428
  117.8 34.8 %copy-start.1 = (bf16[1,22,22,768]{3,2,1,0:T(8,128)(2,1)S(1)}, bf16[1,22,22,768]{3,2,1,0:T(8,128)(2,1)}, u32[]{:S(2)}) copy-start(bf16[1,22,22,768]{3,2,1,0:T(8,128)(2,1)} %param.8) | copy-start | bytes 2230276
  163.3 12.9 %slice-start.2 = ((s8[4718592]{0:T(1024)(128)(4,1)}), s8[4194304]{0:T(1024)(128)(4,1)S(1)}, s32[]{:S(2)}) async-start(s8[4718592]{0:T(1024)(128)(4,1)} %bitcast.101), calls=%async_computation.3 | async-start | bytes 8388608
  174.6 33.5 %collective-permute-start.1 = (bf16[768,3072]{1,0:T(8,128)(2,1)}, bf16[768,3072]{1,0:T(8,128)(2,1)}, u32[]{:S(2)}, u32[]{:S(2)}) collective-permute-start(bf16[768,3072]{1,0:T(8,128)(2,1)} %convolution_convert_fusion.1.refs_1_), channel_id=1, source_target_pairs={{0,16},{16,0},{1,17},{17,1},{2,18},{18,2},{3,19},{19,3},{4,20},{20... | collective-permute-start | bytes 14155784 | tf_op jit(solution)/shard_map/ppermute | solution.py:443
  174.9 33.3 %collective-permute-start.2 = (bf16[3072,768]{1,0:T(8,128)(2,1)}, bf16[3072,768]{1,0:T(8,128)(2,1)}, u32[]{:S(2)}, u32[]{:S(2)}) collective-permute-start(bf16[3072,768]{1,0:T(8,128)(2,1)} %convolution_convert_fusion.refs_2_), channel_id=1, source_target_pairs={{0,16},{16,0},{1,17},{17,1},{2,18},{18,2},{3,19},{19,3},{4,20},{20... | collective-permute-start | bytes 14155784 | tf_op jit(solution)/shard_map/ppermute | solution.py:443
  180.1 19.9 %copy-start.2 = (bf16[22,24,768]{2,1,0:T(8,128)(2,1)S(1)}, bf16[22,24,768]{2,1,0:T(8,128)(2,1)}, u32[]{:S(2)}) copy-start(bf16[22,24,768]{2,1,0:T(8,128)(2,1)} %get-tuple-element.73.cotangent) | copy-start | bytes 2433028
  206.1 1.4 collective-permute-start
  226.3 44.9 %copy-start.8 = (bf16[4,448,128]{2,1,0:T(8,128)(2,1)S(1)}, bf16[4,448,128]{2,1,0:T(8,128)(2,1)}, u32[]{:S(2)}) copy-start(bf16[4,448,128]{2,1,0:T(8,128)(2,1)} %get-tuple-element.43) | copy-start | bytes 1376260
  226.3 53.4 %copy-start.10 = (bf16[4,432,128]{2,1,0:T(8,128)(2,1)S(1)}, bf16[4,432,128]{2,1,0:T(8,128)(2,1)}, u32[]{:S(2)}) copy-start(bf16[4,432,128]{2,1,0:T(8,128)(2,1)} %get-tuple-element.32) | copy-start | bytes 1327108
  226.3 22.8 %collective-permute-start.3 = (bf16[8,432,128]{2,1,0:T(8,128)(2,1)}, bf16[8,432,128]{2,1,0:T(8,128)(2,1)S(1)}, u32[]{:S(2)}, u32[]{:S(2)}) collective-permute-start(bf16[8,432,128]{2,1,0:T(8,128)(2,1)} %get-tuple-element.33), channel_id=1, source_target_pairs={{0,2},{1,3},{2,0},{3,1},{4,6},{5,7},{6,4},{7,5},{8,10},{9,11},{10,... | collective-permute-start | bytes 2654216 | tf_op jit(solution)/shard_map/ppermute | solution.py:340
  227.8 23.7 %collective-permute-start.8 = (bf16[8,432,128]{2,1,0:T(8,128)(2,1)}, bf16[8,432,128]{2,1,0:T(8,128)(2,1)S(1)}, u32[]{:S(2)}, u32[]{:S(2)}) collective-permute-start(bf16[8,432,128]{2,1,0:T(8,128)(2,1)} %get-tuple-element.36), channel_id=1, source_target_pairs={{0,1},{1,0},{2,3},{3,2},{4,5},{5,4},{6,7},{7,6},{8,9},{9,8},{10,11... | collective-permute-start | bytes 2654216 | tf_op jit(solution)/shard_map/ppermute | solution.py:340
  228.4 40.4 %collective-permute-start.13 = (bf16[8,448,128]{2,1,0:T(8,128)(2,1)}, bf16[8,448,128]{2,1,0:T(8,128)(2,1)S(1)}, u32[]{:S(2)}, u32[]{:S(2)}) collective-permute-start(bf16[8,448,128]{2,1,0:T(8,128)(2,1)} %get-tuple-element.39), channel_id=1, source_target_pairs={{0,2},{1,3},{2,0},{3,1},{4,6},{5,7},{6,4},{7,5},{8,10},{9,11},{10,... | collective-permute-start | bytes 2752520 | tf_op jit(solution)/shard_map/ppermute | solution.py:340
  229.6 41.6 %collective-permute-start.18 = (bf16[8,448,128]{2,1,0:T(8,128)(2,1)}, bf16[8,448,128]{2,1,0:T(8,128)(2,1)S(1)}, u32[]{:S(2)}, u32[]{:S(2)}) collective-permute-start(bf16[8,448,128]{2,1,0:T(8,128)(2,1)} %get-tuple-element.42), channel_id=1, source_target_pairs={{0,1},{1,0},{2,3},{3,2},{4,5},{5,4},{6,7},{7,6},{8,9},{9,8},{10,11... | collective-permute-start | bytes 2752520 | tf_op jit(solution)/shard_map/ppermute | solution.py:340
  250.2 29.5 %collective-permute-start.4 = (bf16[4,432,128]{2,1,0:T(8,128)(2,1)S(1)}, bf16[4,432,128]{2,1,0:T(8,128)(2,1)S(1)}, u32[]{:S(2)}, u32[]{:S(2)}) collective-permute-start(bf16[4,432,128]{2,1,0:T(8,128)(2,1)S(1)} %add_convert_fusion.3), channel_id=1, source_target_pairs={{0,1},{1,0},{2,3},{3,2},{4,5},{5,4},{6,7},{7,6},{8,9},{9,8},{10,11... | collective-permute-start | bytes 1327112 | tf_op jit(solution)/shard_map/ppermute | solution.py:340
  252.7 31.7 %copy-start.9 = (bf16[4,432,128]{2,1,0:T(8,128)(2,1)S(1)}, bf16[4,432,128]{2,1,0:T(8,128)(2,1)}, u32[]{:S(2)}) copy-start(bf16[4,432,128]{2,1,0:T(8,128)(2,1)} %get-tuple-element.35) | copy-start | bytes 1327108
  252.7 29.7 %collective-permute-start.9 = (bf16[4,432,128]{2,1,0:T(8,128)(2,1)S(1)}, bf16[4,432,128]{2,1,0:T(8,128)(2,1)S(1)}, u32[]{:S(2)}, u32[]{:S(2)}) collective-permute-start(bf16[4,432,128]{2,1,0:T(8,128)(2,1)S(1)} %add_convert_fusion.2), channel_id=1, source_target_pairs={{0,2},{1,3},{2,0},{3,1},{4,6},{5,7},{6,4},{7,5},{8,10},{9,11},{10,... | collective-permute-start | bytes 1327112 | tf_op jit(solution)/shard_map/ppermute | solution.py:340
  269.9 18.6 %collective-permute-start.14 = (bf16[4,448,128]{2,1,0:T(8,128)(2,1)S(1)}, bf16[4,448,128]{2,1,0:T(8,128)(2,1)S(1)}, u32[]{:S(2)}, u32[]{:S(2)}) collective-permute-start(bf16[4,448,128]{2,1,0:T(8,128)(2,1)S(1)} %add_convert_fusion.1), channel_id=1, source_target_pairs={{0,1},{1,0},{2,3},{3,2},{4,5},{5,4},{6,7},{7,6},{8,9},{9,8},{10,11... | collective-permute-start | bytes 1376264 | tf_op jit(solution)/shard_map/ppermute | solution.py:340
  271.3 19.2 %collective-permute-start.19 = (bf16[4,448,128]{2,1,0:T(8,128)(2,1)S(1)}, bf16[4,448,128]{2,1,0:T(8,128)(2,1)S(1)}, u32[]{:S(2)}, u32[]{:S(2)}) collective-permute-start(bf16[4,448,128]{2,1,0:T(8,128)(2,1)S(1)} %add_convert_fusion), channel_id=1, source_target_pairs={{0,2},{1,3},{2,0},{3,1},{4,6},{5,7},{6,4},{7,5},{8,10},{9,11},{10,... | collective-permute-start | bytes 1376264 | tf_op jit(solution)/shard_map/ppermute | solution.py:340
  279.9 11.6 %collective-permute-start.7 = (bf16[432,128]{1,0:T(8,128)(2,1)S(1)}, bf16[432,128]{1,0:T(8,128)(2,1)S(1)}, u32[]{:S(2)}, u32[]{:S(2)}) collective-permute-start(bf16[432,128]{1,0:T(8,128)(2,1)S(1)} %get-tuple-element.86), channel_id=1, source_target_pairs={{0,12},{1,13},{2,14},{3,15},{4,8},{5,9},{6,10},{7,11},{8,4},{9,5},... | collective-permute-start | bytes 331784 | tf_op jit(solution)/shard_map/ppermute | solution.py:340
  281.7 11.8 %collective-permute-start.6 = (bf16[432,128]{1,0:T(8,128)(2,1)S(1)}, bf16[432,128]{1,0:T(8,128)(2,1)S(1)}, u32[]{:S(2)}, u32[]{:S(2)}) collective-permute-start(bf16[432,128]{1,0:T(8,128)(2,1)S(1)} %get-tuple-element.87), channel_id=1, source_target_pairs={{0,8},{1,9},{2,10},{3,11},{4,12},{5,13},{6,14},{7,15},{8,0},{9,1},... | collective-permute-start | bytes 331784 | tf_op jit(solution)/shard_map/ppermute | solution.py:340
  282.4 12.8 %collective-permute-start.5 = (bf16[432,128]{1,0:T(8,128)(2,1)S(1)}, bf16[432,128]{1,0:T(8,128)(2,1)S(1)}, u32[]{:S(2)}, u32[]{:S(2)}) collective-permute-start(bf16[432,128]{1,0:T(8,128)(2,1)S(1)} %get-tuple-element.85), channel_id=1, source_target_pairs={{0,4},{1,5},{2,6},{3,7},{4,0},{5,1},{6,2},{7,3},{8,12},{9,13},{10,... | collective-permute-start | bytes 331784 | tf_op jit(solution)/shard_map/ppermute | solution.py:340
  288.5 7.8 %collective-permute-start.12 = (bf16[432,128]{1,0:T(8,128)(2,1)S(1)}, bf16[432,128]{1,0:T(8,128)(2,1)S(1)}, u32[]{:S(2)}, u32[]{:S(2)}) collective-permute-start(bf16[432,128]{1,0:T(8,128)(2,1)S(1)} %get-tuple-element.83), channel_id=1, source_target_pairs={{0,12},{1,13},{2,14},{3,15},{4,8},{5,9},{6,10},{7,11},{8,4},{9,5},... | collective-permute-start | bytes 331784 | tf_op jit(solution)/shard_map/ppermute | solution.py:340
  290.5 17.5 %collective-permute-start.11 = (bf16[432,128]{1,0:T(8,128)(2,1)S(1)}, bf16[432,128]{1,0:T(8,128)(2,1)S(1)}, u32[]{:S(2)}, u32[]{:S(2)}) collective-permute-start(bf16[432,128]{1,0:T(8,128)(2,1)S(1)} %get-tuple-element.84), channel_id=1, source_target_pairs={{0,8},{1,9},{2,10},{3,11},{4,12},{5,13},{6,14},{7,15},{8,0},{9,1},... | collective-permute-start | bytes 331784 | tf_op jit(solution)/shard_map/ppermute | solution.py:340
  291.5 16.8 %collective-permute-start.10 = (bf16[432,128]{1,0:T(8,128)(2,1)S(1)}, bf16[432,128]{1,0:T(8,128)(2,1)S(1)}, u32[]{:S(2)}, u32[]{:S(2)}) collective-permute-start(bf16[432,128]{1,0:T(8,128)(2,1)S(1)} %get-tuple-element.82), channel_id=1, source_target_pairs={{0,4},{1,5},{2,6},{3,7},{4,0},{5,1},{6,2},{7,3},{8,12},{9,13},{10,... | collective-permute-start | bytes 331784 | tf_op jit(solution)/shard_map/ppermute | solution.py:340
  293.5 14.8 %collective-permute-start.17 = (bf16[448,128]{1,0:T(8,128)(2,1)S(1)}, bf16[448,128]{1,0:T(8,128)(2,1)S(1)}, u32[]{:S(2)}, u32[]{:S(2)}) collective-permute-start(bf16[448,128]{1,0:T(8,128)(2,1)S(1)} %get-tuple-element.78), channel_id=1, source_target_pairs={{0,12},{1,13},{2,14},{3,15},{4,8},{5,9},{6,10},{7,11},{8,4},{9,5},... | collective-permute-start | bytes 344072 | tf_op jit(solution)/shard_map/ppermute | solution.py:340
  295.3 21.0 %collective-permute-start.16 = (bf16[448,128]{1,0:T(8,128)(2,1)S(1)}, bf16[448,128]{1,0:T(8,128)(2,1)S(1)}, u32[]{:S(2)}, u32[]{:S(2)}) collective-permute-start(bf16[448,128]{1,0:T(8,128)(2,1)S(1)} %get-tuple-element.79), channel_id=1, source_target_pairs={{0,8},{1,9},{2,10},{3,11},{4,12},{5,13},{6,14},{7,15},{8,0},{9,1},... | collective-permute-start | bytes 344072 | tf_op jit(solution)/shard_map/ppermute | solution.py:340
  296.3 19.9 %collective-permute-start.15 = (bf16[448,128]{1,0:T(8,128)(2,1)S(1)}, bf16[448,128]{1,0:T(8,128)(2,1)S(1)}, u32[]{:S(2)}, u32[]{:S(2)}) collective-permute-start(bf16[448,128]{1,0:T(8,128)(2,1)S(1)} %get-tuple-element.77), channel_id=1, source_target_pairs={{0,4},{1,5},{2,6},{3,7},{4,0},{5,1},{6,2},{7,3},{8,12},{9,13},{10,... | collective-permute-start | bytes 344072 | tf_op jit(solution)/shard_map/ppermute | solution.py:340
  308.0 8.3 %collective-permute-start.22 = (bf16[448,128]{1,0:T(8,128)(2,1)S(1)}, bf16[448,128]{1,0:T(8,128)(2,1)S(1)}, u32[]{:S(2)}, u32[]{:S(2)}) collective-permute-start(bf16[448,128]{1,0:T(8,128)(2,1)S(1)} %get-tuple-element.75), channel_id=1, source_target_pairs={{0,12},{1,13},{2,14},{3,15},{4,8},{5,9},{6,10},{7,11},{8,4},{9,5},... | collective-permute-start | bytes 344072 | tf_op jit(solution)/shard_map/ppermute | solution.py:340
  308.3 11.7 %collective-permute-start.21 = (bf16[448,128]{1,0:T(8,128)(2,1)S(1)}, bf16[448,128]{1,0:T(8,128)(2,1)S(1)}, u32[]{:S(2)}, u32[]{:S(2)}) collective-permute-start(bf16[448,128]{1,0:T(8,128)(2,1)S(1)} %get-tuple-element.76), channel_id=1, source_target_pairs={{0,8},{1,9},{2,10},{3,11},{4,12},{5,13},{6,14},{7,15},{8,0},{9,1},... | collective-permute-start | bytes 344072 | tf_op jit(solution)/shard_map/ppermute | solution.py:340
  308.3 17.0 %copy-start = (f32[3496,128]{1,0:T(8,128)S(1)}, f32[3496,128]{1,0:T(8,128)}, u32[]{:S(2)}) copy-start(f32[3496,128]{1,0:T(8,128)} %param.9) | copy-start | bytes 5369860
  308.4 11.6 %collective-permute-start.20 = (bf16[448,128]{1,0:T(8,128)(2,1)S(1)}, bf16[448,128]{1,0:T(8,128)(2,1)S(1)}, u32[]{:S(2)}, u32[]{:S(2)}) collective-permute-start(bf16[448,128]{1,0:T(8,128)(2,1)S(1)} %get-tuple-element.74), channel_id=1, source_target_pairs={{0,4},{1,5},{2,6},{3,7},{4,0},{5,1},{6,2},{7,3},{8,12},{9,13},{10,... | collective-permute-start | bytes 344072 | tf_op jit(solution)/shard_map/ppermute | solution.py:340
  320.9 3.2 collective-permute-start.23
  (12 other events, 70.2 us)
Sparse Core Ops, SparseCore 0:
  11.4 106.3 all-gather.1

commit v2 on v1

--- a/solution.py
+++ b/solution.py
@@ -6,6 +6,7 @@
 from jax.experimental import pallas as pl
 from jax.experimental.pallas import tpu as pltpu
 from jax.sharding import PartitionSpec as P
+
 
 C = 768
 FF = 3072
@@ -24,7 +25,8 @@
 OUT_AT = BIN_AT + FF_ROWS
 TAIL_AT = OUT_AT + FF * C_ROWS
 P_ROWS = TAIL_AT + 2 * C_ROWS
-SMALL = 64
+SMALL = 8
+HEAD_PAD = 56
 STEPS = 6
 IN_COLS = FF // STEPS
 OUT_ROWS = FF // STEPS
@@ -166,7 +168,7 @@
         unmix_body,
         out_shape=[
             jax.ShapeDtypeStruct((SIDE, WIDE, C), BF16),
-            jax.ShapeDtypeStruct((SMALL, C), F32),
+            jax.ShapeDtypeStruct((HEAD_PAD, C), F32),
         ],
         scratch_shapes=[
             pltpu.VMEM((SIDE + 2 * REACH, 40, LANES), F32),
@@ -201,9 +203,8 @@
     def _():
         for j in range(C_ROWS):
             lane = slice(j * LANES, (j + 1) * LANES)
-            small[0:HEAD, lane] = flat[pl.ds(j, HEAD, stride=C_ROWS), :]
-            small[HEAD : HEAD + 4, lane] = flat[pl.ds(BIN_AT + j, 4, stride=C_ROWS), :]
-            small[HEAD + 4 : HEAD + 6, lane] = flat[pl.ds(TAIL_AT + j, 2, stride=C_ROWS), :]
+            small[0:4, lane] = flat[pl.ds(BIN_AT + j, 4, stride=C_ROWS), :]
+            small[4:6, lane] = flat[pl.ds(TAIL_AT + j, 2, stride=C_ROWS), :]
 
     @pl.when(step >= owners)
     def _():
@@ -268,9 +269,9 @@
     def _():
         for j in range(C_ROWS):
             lane = slice(j * LANES, (j + 1) * LANES)
-            flat[pl.ds(j, HEAD, stride=C_ROWS), :] = small[0:HEAD, lane]
-            flat[pl.ds(BIN_AT + j, 4, stride=C_ROWS), :] = small[HEAD : HEAD + 4, lane]
-            flat[pl.ds(TAIL_AT + j, 2, stride=C_ROWS), :] = small[HEAD + 4 : HEAD + 6, lane]
+            flat[pl.ds(BIN_AT + j, 4, stride=C_ROWS), :] = small[0:4, lane]
+            flat[pl.ds(TAIL_AT + j, 2, stride=C_ROWS), :] = small[4:6, lane]
+        flat[0:IN_AT, :] = jnp.zeros((IN_AT, LANES), F32)
         flat[P_ROWS : P_ROWS + MARGIN, :] = jnp.zeros((MARGIN, LANES), F32)
 
     @pl.when(step < STEPS)
@@ -340,21 +341,42 @@
     return lax.ppermute(value, "fsdp", [(i, i ^ mask) for i in range(size)])
 
 
-def reduce_part(far, near, home, masks, size):
+def sum_small(value, size):
+    mask = 1
+    while mask < size:
+        value = add(value, swap(value, mask, size)).astype(BF16)
+        mask *= 2
+    return value
+
+
+def replica_others(value, replicas):
+    turn = lambda k: [(i, (i + k) % replicas) for i in range(replicas)]
+    return [lax.ppermute(value, "dp", turn(k)) for k in range(1, replicas)]
+
+
+def first_phase(far, near, home, masks, size):
     got = swap(far, masks[0], size)
     half = near.shape[0]
-    near = add(near, got[half:]).astype(BF16)
-    back = swap(near, masks[1], size)
-    home = add(home, got[:half], back)
+    return add(near, got[half:]).astype(BF16), add(home, got[:half])
+
+
+def second_phase(near, home, masks, size):
+    return home + swap(near, masks[1], size).astype(F32)
+
+
+def last_phase(home, shift, size):
     low = home.astype(BF16)
-    pieces = [swap(low[k], 4 * k, size) for k in (1, 2, 3)]
+    pieces = [swap(low[k], k * shift, size) for k in (1, 2, 3)]
     return add(home[0], *pieces).astype(BF16)
 
 
-def image_pass(image, cot_image, small, weight_in, weight_out):
-    bias_in = small[HEAD : HEAD + 4].reshape(-1)
-    bias_out, layer_scale = small[HEAD + 4], small[HEAD + 5]
-    normed, scaled, inverse = mix(image, small)
+def after(value, gates):
+    return lax.optimization_barrier((value, *gates))[0]
+
+
+def forward_backward(normed, cot_image, small, weight_in, weight_out):
+    bias_in = small[0:4].reshape(-1)
+    bias_out, layer_scale = small[4], small[5]
     normed_low = normed.reshape(-1, C)
     before = jnp.dot(normed_low, weight_in, preferred_element_type=F32) + bias_in
     activated = (before * 0.5 * (1.0 + lax.erf(before * ROOT_HALF))).astype(BF16)
@@ -381,19 +403,15 @@
     normed_grad = lax.dot_general(
         before_grad, weight_in, (((1,), (1,)), ((), ())), preferred_element_type=F32
     )
-    result, head_grad = unmix(
-        image, cot_image, small, normed_grad.reshape(SIDE, WIDE, C), scaled, inverse
-    )
     small_grad = jnp.concatenate(
         [
-            head_grad[:HEAD],
             grad_bias_in.reshape(-1, C),
             grad_bias_out[None],
             grad_scale[None],
-            jnp.zeros((SMALL - HEAD - 6, C), F32),
+            jnp.zeros((SMALL - 6, C), F32),
         ]
     ).astype(BF16)
-    return small_grad, grad_weight_in, grad_weight_out, result
+    return small_grad, grad_weight_in, grad_weight_out, normed_grad.reshape(normed.shape)
 
 
 def adam_update(gradient, weights, first, second_moment):
@@ -404,7 +422,7 @@
     return (weights_new, first_new, second_new)
 
 
-def per_device(images_in, cotangent, master, moment, second, owner, offset):
+def device_step(images_in, cotangent, master, moment, second, owner, offset):
     owners = lax.axis_size("fsdp")
     replicas = lax.axis_size("dp")
     me = lax.axis_index("fsdp")
@@ -423,8 +441,22 @@
     chosen = rank[None, :] == ids[:, None]
     pick = lambda mask, values: jnp.sum(jnp.where(mask, values[None, :], 0), 1)
 
+    mine_start = jnp.sum(jnp.where(ids == me, starts, 0))
+    mine_count = jnp.sum(jnp.where(ids == me, counts, 0))
+    head_shift = jnp.minimum(mine_start, IN_AT)
+
     lowered = jnp.pad(master, ((0, replicas * rows - bucket), (0, 0))).astype(BF16)
     mine = lax.dynamic_slice_in_dim(lowered, core * rows, rows, 0)
+    head_from = jnp.concatenate([jnp.zeros((IN_AT, LANES), BF16), lowered[:IN_AT]])
+    head_mine = lax.dynamic_slice_in_dim(head_from, IN_AT - head_shift, IN_AT, 0)
+    held = jnp.arange(IN_AT)[:, None] < mine_start + mine_count
+    head = sum_small(jnp.where(held, head_mine, jnp.zeros_like(head_mine)), owners)
+    head = jnp.pad(head.astype(F32).reshape(HEAD, C), ((0, HEAD_PAD - HEAD), (0, 0)))
+
+    widen = lambda value: jnp.pad(value[0], ((0, 0), (0, WIDE - SIDE), (0, 0)))
+    image, cot_image = widen(images_in), widen(cotangent)
+    normed, scaled, inverse = mix(image, head)
+
     gathered = lax.all_gather(mine, ("dp", "fsdp"), axis=0, tiled=True)
     small, weight_in, weight_out = unpack(
         gathered.reshape(replicas, owners * rows, LANES),
@@ -432,36 +464,47 @@
         pick(chosen, starts),
         pick(chosen, counts),
     )
-
-    widen = lambda value: jnp.pad(value[0], ((0, 0), (0, WIDE - SIDE), (0, 0)))
-    small_grad, grad_in, grad_out, result = image_pass(
-        widen(images_in), widen(cotangent), small, weight_in, weight_out
-    )
-    input_grad = result[None, :, :SIDE]
+    small_grad, grad_in, grad_out, normed_grad = forward_backward(
+        normed, cot_image, small, weight_in, weight_out
+    )
 
     if replicas == 2 and owners == 16:
         other = lambda value: lax.ppermute(value, "dp", [(0, 1), (1, 0)])
         far_out, far_in, far_small = other(grad_out), other(grad_in), other(small_grad)
-        quarter = rows // 32 * 8 // 16 * 16
-        sizes = [quarter, quarter, rows // 2 - quarter, rows // 2 - quarter]
+        cross = rows * 9 // 64 // 32 * 32
+        wide = -(-(rows - cross) // 4) // 16 * 16
+        slim = (rows - cross) // 2 - wide
         groups = []
         at = 0
-        for number, size in enumerate(sizes):
+        for number, size in enumerate((wide, slim, wide, slim)):
             groups += [(number % 2, f, c, at, size) for f, c in ((8, 8), (4, 4), (0, 4))]
             at += size
+        groups += [(2, 4 * k, 4, at, cross) for k in range(4)]
         spots = jnp.arange(16, dtype=jnp.int32)
         high, low, deep = spots >> 3, (spots >> 2) & 1, spots & 3
-        tables = [deep * 4 + high * 2 + low, deep * 4 + low * 2 + high]
+        tables = [deep * 4 + high * 2 + low, deep * 4 + low * 2 + high, spots]
         bases = jnp.concatenate(
             [pick((table ^ me)[:, None] == ids[None, :], starts) for table in tables]
         ) + core * rows
         packed = pack(
             bases, add(small_grad, far_small), (grad_in, far_in), (grad_out, far_out), owners, groups
         )
-        sums = [
-            reduce_part(*packed[3 * k : 3 * k + 3], (2, 1) if k % 2 == 0 else (1, 2), owners)
-            for k in range(4)
-        ]
+        normed_grad, packed = lax.optimization_barrier((normed_grad, packed))
+        masks = [(2, 1), (1, 2)]
+        home, *away = packed[12:]
+        across = [swap(away[k - 1], 4 * k, owners) for k in (1, 2, 3)]
+        sums, gates, behind = [], [], ()
+        for chunk in range(2):
+            firsts = []
+            for k in range(2):
+                far, near, kept = packed[6 * chunk + 3 * k : 6 * chunk + 3 * k + 3]
+                far = after(far, behind) if behind else far
+                firsts.append(first_phase(far, near, kept, masks[k], owners))
+            behind = tuple(value[0] for value in firsts)
+            seconds = [second_phase(*firsts[k], masks[k], owners) for k in range(2)]
+            sums.append(last_phase(jnp.concatenate(seconds, 1), 4, owners))
+            gates = [behind, tuple(seconds)]
+        sums.append(last_phase(add(home, *across), 1, owners))
         half = jnp.concatenate(sums, 0)
         theirs = other(half)
         grad_low = jnp.where(
@@ -475,9 +518,24 @@
         half = lax.psum_scatter(part, "fsdp", scatter_dimension=0, tiled=True)
         grad_low = lax.all_gather(half, "dp", axis=0, tiled=True)
 
-    mine_count = jnp.sum(jnp.where(ids == me, counts, 0))
-    valid = jnp.arange(bucket)[:, None] < mine_count
-    grad_full = jnp.where(valid, grad_low[:bucket].astype(F32), 0.0)
+    result, head_grad = unmix(image, cot_image, head, normed_grad, scaled, inverse)
+    input_grad = result[None, :, :SIDE]
+    head_low = head_grad[:HEAD].astype(BF16).reshape(IN_AT, LANES)
+    head_low = add(head_low, *replica_others(head_low, replicas)).astype(BF16)
+    if replicas == 2 and owners == 16:
+        for shift, gate in zip((1, 4), gates, strict=True):
+            head_low = after(head_low, gate)
+            head_low = add(head_low, *[swap(head_low, k * shift, owners) for k in (1, 2, 3)]).astype(BF16)
+    else:
+        head_low = sum_small(head_low, owners)
+    head_to = jnp.concatenate([head_low, jnp.zeros((IN_AT, LANES), BF16)])
+    head_rows = lax.dynamic_slice_in_dim(head_to, head_shift, IN_AT, 0)
+    slot = jnp.arange(bucket)[:, None]
+    grad_low = jnp.where(
+        slot < IN_AT - head_shift, jnp.pad(head_rows, ((0, bucket - IN_AT), (0, 0))), grad_low[:bucket]
+    )
+    grad_low = lax.optimization_barrier(grad_low)
+    grad_full = jnp.where(slot < mine_count, grad_low.astype(F32), 0.0)
     new_master, new_moment, new_second = adam_update(grad_full, master, moment, second)
     return (input_grad, new_master, new_moment, new_second)
 
@@ -493,7 +551,7 @@
         P(),
     )
     return jax.shard_map(
-        per_device,
+        device_step,
         mesh=mesh,
         in_specs=placed,
         out_specs=(

time: 337 us -> 333 us (0.988)
  waiting for transfers between devices: 165 us -> 131 us
  starting transfers between devices: 29.6 us -> 46 us
  other arithmetic: 17.4 us -> 27.1 us
  matrix products: 31.6 us -> 35 us
    all_gather x1, waiting for transfers between devices: 104 us -> 64.7 us  [device_step(): gathered = lax.all_gather(mine, ('dp', 'fsdp'), axis=0, tiled=True)]
    ppermute x20 -> x30, starting transfers between devices: 28.7 us -> 45 us  [swap(): return lax.ppermute(value, 'fsdp', [(i, i ^ mask) for i in range(size)])]
    select_n x1 -> x3, other arithmetic: 0.02 us -> 14.1 us  [the longest x1 13.9 us: device_step(): jnp.where(slot < IN_AT - head_shift, jnp.pad(head_rows, ((0, bucket - IN_...]
    ppermute x20 -> x30, waiting for transfers between devices: 60.2 us -> 66 us  [swap(): return lax.ppermute(value, 'fsdp', [(i, i ^ mask) for i in range(size)])]
    dot_general x6, matrix products: 31.6 us -> 35 us  [the longest x1 7.2 us: forward_backward(): lax.dot_general(before_grad, weight_in, (((1,), (1,)), ((), ())), preferr...]
  transfers between devices with their start and end apart: 25 -> 36, of which waited for: 10 -> 18; matrix products, arithmetic and copies ran while one was open for 7% -> 7% of each run, Pallas kernels for 6% -> 10%
where the time goes in v2:
time: 333 us; the launch traced here: 332 us
  waiting for transfers between devices  131 us (39%)
  Pallas kernels  70.8 us (21%)
  starting transfers between devices  46 us (14%)
  matrix products  35 us (11%)
  other arithmetic  27.1 us (8%)
  between operations  16.6 us (5%)
  local copies, waits for them, and re-layouts  5.95 us (2%)
    ppermute x30, waiting for transfers between devices, swap(): return lax.ppermute(value, 'fsdp', [(i, i ^ mask) for i in range(size)])  66 us
    all_gather x1, waiting for transfers between devices, device_step(): gathered = lax.all_gather(mine, ('dp', 'fsdp'), axis=0, tiled=True)  64.7 us
    ppermute x30, starting transfers between devices, swap(): return lax.ppermute(value, 'fsdp', [(i, i ^ mask) for i in range(size)])  45 us
    pallas_call x1, Pallas kernels, unmix(): pl.pallas_call(unmix_body, out_shape=[jax.ShapeDtypeStruct((SIDE, WIDE, C...  19.1 us
    pallas_call x1, Pallas kernels, pack(): pl.pallas_call(functools.partial(pack_body, paired, groups, owners), grid...  18.5 us
    pallas_call x1, Pallas kernels, unpack(): pl.pallas_call(functools.partial(unpack_body, parts, rows, owners), grid_...  18.2 us
    pallas_call x1, Pallas kernels, mix(): pl.pallas_call(mix_body, out_shape=[jax.ShapeDtypeStruct((SIDE, WIDE, C),...  15 us
    select_n x1, other arithmetic, device_step(): jnp.where(slot < IN_AT - head_shift, jnp.pad(head_rows, ((0, bucket - IN_...  13.9 us
  transfers between devices with their start and end apart: 36, of which 18 were waited for; matrix products, arithmetic and copies ran while one was open for 7% of the time, Pallas kernels for 10%

profile of v2, /device:TPU:0, one launch (start us, length us, event | category | flops | bytes accessed | tf_op | source)
XLA Modules:
  0.0 332.3 jit_solution(15103305166159546617)
XLA Ops:
  13.5 3.0 collective-permute-start
  16.6 2.4 collective-permute-done
  21.3 2.4 collective-permute-done.1
  26.8 3.3 collective-permute-done.2
  30.1 2.8 collective-permute-start.3
  33.6 6.6 %collective-permute-done.3 = bf16[312,128]{1,0:T(8,128)(2,1)S(1)} collective-permute-done((bf16[312,128]{1,0:T(8,128)(2,1)S(1)}, bf16[312,128]{1,0:T(8,128)(2,1)S(1)}, u32[]{:S(2)}, u32[]{:S(2)}) %collective-permute-start.3) | collective-permute-done | bytes 79904 | tf_op jit(solution)/shard_map/ppermute | solution.py:341
  41.0 15.0 %mix.1 = (bf16[22,24,768]{2,1,0:T(8,128)(2,1)}, f32[22,24,768]{2,1,0:T(8,128)}, f32[22,24,128]{2,1,0:T(8,128)}) custom-call(bf16[22,24,768]{2,1,0:T(8,128)(2,1)} %pad.24.image, f32[56,768]{1,0:T(8,128)} %pad_convert_fusion.small), custom_call_target="tpu_custom_call" | custom-call | tf_op jit(solution)/shard_map/mix/pallas_call | solution.py:95
  56.0 64.7 %all-gather.2.cloned.1.call-done = bf16[56320,128]{1,0:T(8,128)(2,1)} async-done(((bf16[1760,128]{1,0:T(8,128)(2,1)}), bf16[56320,128]{1,0:T(8,128)(2,1)}) %all-gather.2.cloned.1.call-update) | async-done | bytes 14417936 | tf_op jit(solution)/shard_map/all_gather | solution.py:460
  120.7 18.2 %unpack.1 = (f32[8,768]{1,0:T(8,128)}, bf16[768,3072]{1,0:T(8,128)(2,1)}, bf16[3072,768]{1,0:T(8,128)(2,1)}) custom-call(s32[16]{0:T(128)} %get-tuple-element.103.order, s32[16]{0:T(128)} %get-tuple-element.102.starts, s32[16]{0:T(128)} %get-tuple-element.101.counts, bf16[2,28160,128]{2,1,0:T(8,128)(2,1)} %bitcast.74), custom_call_target="tpu_custom_call" | custom-call | tf_op jit(solution)/shard_map/unpack/pallas_call | solution.py:241
  140.7 5.5 %multiply_convert_fusion = (bf16[528,3072]{1,0:T(8,128)(2,1)S(1)}, f32[528,3072]{1,0:T(8,128)S(1)}) fusion(f32[3072]{0:T(1024)S(1)} %add.215, bf16[528,768]{1,0:T(8,128)(2,1)S(1)} %bitcast.81, bf16[768,3072]{1,0:T(8,128)(2,1)} %get-tuple-element.52), kind=kOutput, calls=%fused_computation.7 | convolution fusion | flops 2501148672 | bytes 15273984 | tf_op jit(solution)/shard_map/dot_general | solution.py:381
  146.3 4.7 %fusion.44 = (bf16[3072]{0:T(1024)(128)(2,1)S(1)}, bf16[528,3072]{1,0:T(8,128)(2,1)S(1)}) fusion(f32[528,3072]{1,0:T(8,128)S(1)} %get-tuple-element.124, f32[3072]{0:T(1024)S(1)} %add.215, bf16[528,768]{1,0:T(8,128)(2,1)S(1)} %fusion.8, bf16[3072,768]{1,0:T(8,128)(2,1)S(1)} %bitcast.80), kind=kOutput, calls=%fused_computation.129 | convolution fusion | flops 2510877696 | bytes 15280128 | tf_op jit(solution)/shard_map/dot_general | solution.py:391
  151.0 5.6 %convolution_convert_fusion.1.refs_1_ = bf16[768,3072]{1,0:T(8,128)(2,1)} fusion(bf16[528,768]{1,0:T(8,128)(2,1)S(1)} %bitcast.82, bf16[528,3072]{1,0:T(8,128)(2,1)S(1)} %get-tuple-element.126), kind=kOutput, calls=%fused_computation.10 | convolution fusion | flops 2493775872 | bytes 8773632 | tf_op jit(solution)/shard_map/dot_general | solution.py:400
  156.7 5.7 %convolution_convert_fusion.refs_2_ = bf16[3072,768]{1,0:T(8,128)(2,1)} fusion(bf16[528,3072]{1,0:T(8,128)(2,1)S(1)} %get-tuple-element.123, bf16[528,768]{1,0:T(8,128)(2,1)S(1)} %fusion.8), kind=kOutput, calls=%fused_computation.9 | convolution fusion | flops 2493775872 | bytes 8773632 | tf_op jit(solution)/shard_map/dot_general | solution.py:388
  163.8 6.3 %fusion.9 = bf16[768]{0:T(1024)(128)(2,1)S(1)} fusion(bf16[22,24,768]{2,1,0:T(8,128)(2,1)S(1)} %get-tuple-element.112.cotangent, bf16[528,3072]{1,0:T(8,128)(2,1)} %copy-done.25, bf16[3072,768]{1,0:T(8,128)(2,1)} %get-tuple-element.50, f32[768]{0:T(1024)S(1)} %get-tuple-element.94), kind=kOutput, calls=%fused_computation.29 | convolution fusion | flops 2493037824 | bytes 8778240 | tf_op jit(solution)/shard_map/dot_general | solution.py:383
  170.5 7.2 %fusion.45 = f32[528,768]{1,0:T(8,128)} fusion(bf16[528,3072]{1,0:T(8,128)(2,1)} %copy-done.26, bf16[768,3072]{1,0:T(8,128)(2,1)} %get-tuple-element.52), kind=kOutput, calls=%fused_computation.130 | convolution fusion | flops 2491416576 | bytes 9584640 | tf_op jit(solution)/shard_map/dot_general | solution.py:403
  178.4 18.5 %pack.1 = (bf16[8,384,128]{2,1,0:T(8,128)(2,1)}, bf16[4,384,128]{2,1,0:T(8,128)(2,1)}, bf16[4,384,128]{2,1,0:T(8,128)(2,1)}, bf16[8,384,128]{2,1,0:T(8,128)(2,1)...) custom-call(s32[48]{0:T(128)} %add_add_fusion.bases, ...), custom_call_target="tpu_custom_call" | custom-call | tf_op jit(solution)/shard_map/pack/pallas_call | solution.py:323
  198.4 19.1 %unmix.1 = (bf16[22,24,768]{2,1,0:T(8,128)(2,1)}, f32[56,768]{1,0:T(8,128)}) custom-call(bf16[22,24,768]{2,1,0:T(8,128)(2,1)} %pad.24.image, bf16[22,24,768]{2,1,0:T(8,128)(2,1)} %copy-done.2, f32[56,768]{1,0:T(8,128)} %pad_convert_fusion.small, f32[22,24,768]{2,1,0:T(8,128)} %bitcast.77, f32[22,24,768]{2,1,0:T(8,128)} %get-tuple-element.70.scaled, ...), custom_call_target="tpu_custom_call" | custom-call | tf_op jit(solution)/shard_map/unmix/pallas_call | solution.py:167
  224.4 5.4 %collective-permute-done.30 = bf16[4,224,128]{2,1,0:T(8,128)(2,1)S(1)} collective-permute-done((bf16[4,224,128]{2,1,0:T(8,128)(2,1)S(1)}, bf16[4,224,128]{2,1,0:T(8,128)(2,1)S(1)}, u32[]{:S(2)}, u32[]{:S(2)}) %collective-permute-start.30) | collective-permute-done | bytes 229408 | tf_op jit(solution)/shard_map/ppermute | solution.py:341
  229.8 12.7 %collective-permute-done.29 = bf16[4,224,128]{2,1,0:T(8,128)(2,1)S(1)} collective-permute-done((bf16[4,224,128]{2,1,0:T(8,128)(2,1)S(1)}, bf16[4,224,128]{2,1,0:T(8,128)(2,1)S(1)}, u32[]{:S(2)}, u32[]{:S(2)}) %collective-permute-start.29) | collective-permute-done | bytes 229408 | tf_op jit(solution)/shard_map/ppermute | solution.py:341
  251.7 6.7 %collective-permute-done.20 = bf16[4,384,128]{2,1,0:T(8,128)(2,1)S(1)} collective-permute-done((bf16[4,384,128]{2,1,0:T(8,128)(2,1)S(1)}, bf16[4,384,128]{2,1,0:T(8,128)(2,1)S(1)}, u32[]{:S(2)}, u32[]{:S(2)}) %collective-permute-start.20) | collective-permute-done | bytes 393248 | tf_op jit(solution)/shard_map/ppermute | solution.py:341
  259.5 2.2 collective-permute-start.24
  261.7 2.2 collective-permute-start.22
  264.0 10.0 %collective-permute-done.10 = bf16[8,384,128]{2,1,0:T(8,128)(2,1)S(1)} collective-permute-done((bf16[8,384,128]{2,1,0:T(8,128)(2,1)S(1)}, bf16[8,384,128]{2,1,0:T(8,128)(2,1)S(1)}, u32[]{:S(2)}, u32[]{:S(2)}) %collective-permute-start.10) | collective-permute-done | bytes 786464 | tf_op jit(solution)/shard_map/ppermute | solution.py:341
  279.8 5.0 %collective-permute-done.15 = bf16[4,384,128]{2,1,0:T(8,128)(2,1)S(1)} collective-permute-done((bf16[4,384,128]{2,1,0:T(8,128)(2,1)S(1)}, bf16[4,384,128]{2,1,0:T(8,128)(2,1)S(1)}, u32[]{:S(2)}, u32[]{:S(2)}) %collective-permute-start.15) | collective-permute-done | bytes 393248 | tf_op jit(solution)/shard_map/ppermute | solution.py:341
  286.7 2.2 collective-permute-start.27
  288.9 2.2 collective-permute-start.25
  291.2 2.2 collective-permute-start.19
  293.4 3.0 collective-permute-done.27
  296.4 4.2 %collective-permute-start.17 = (bf16[312,128]{1,0:T(8,128)(2,1)S(1)}, bf16[312,128]{1,0:T(8,128)(2,1)S(1)}, u32[]{:S(2)}, u32[]{:S(2)}) collective-permute-start(bf16[312,128]{1,0:T(8,128)(2,1)S(1)} %add_convert_fusion.5), channel_id=1, source_target_pairs={{0,4},{1,5},{2,6},{3,7},{4,0},{5,1},{6,2},{7,3},{8,12},{9,13},{10,... | collective-permute-start | bytes 239624 | tf_op jit(solution)/shard_map/ppermute | solution.py:341
  300.6 4.9 %collective-permute-done.26 = bf16[768,128]{1,0:T(8,128)(2,1)S(1)} collective-permute-done((bf16[768,128]{1,0:T(8,128)(2,1)S(1)}, bf16[768,128]{1,0:T(8,128)(2,1)S(1)}, u32[]{:S(2)}, u32[]{:S(2)}) %collective-permute-start.26) | collective-permute-done | bytes 196640 | tf_op jit(solution)/shard_map/ppermute | solution.py:341
  307.5 13.9 %fusion.13 = bf16[3496,128]{1,0:T(8,128)(2,1)S(1)} fusion(bf16[1760,128]{1,0:T(8,128)(2,1)S(1)} %collective-permute-done.34, bf16[224,128]{1,0:T(8,128)(2,1)S(1)} %fusion.30, bf16[768,128]{1,0:T(8,128)(2,1)S(1)} %fusion.20, bf16[768,128]{1,0:T(8,128)(2,1)S(1)} %fusion.26, bf16[312,128]{1,0:T(8,128)(2,1)S(1)} %pad_dynamic-slice_fusion.1, ...), kind=kLoop, calls=%fused_computation.35 | loop fusion | flops 8054784 | bytes 1879465 | tf_op jit(solution)/shard_map/jit(_where)/select_n | solution.py:534
  321.4 4.1 %multiply_subtract_fusion = (f32[3496,128]{1,0:T(8,128)}, f32[3496,128]{1,0:T(8,128)}, f32[3496,128]{1,0:T(8,128)}) fusion(f32[3496,128]{1,0:T(8,128)S(1)} %copy-done, bf16[3496,128]{1,0:T(8,128)(2,1)S(1)} %fusion.13, pred[3496]{0:T(1024)(128)(4,1)S(1)} %iota_compare_fusion.2, f32[3496,128]{1,0:T(8,128)S(1)} %copy-done.3, f32[3496,128]{1,0:T(8,128)S(1)} %copy-done.4), kind=kLoop, calls=%fused_computation.21 | loop fusion | flops 7159808 | bytes 11638184 | tf_op jit(solution)/shard_map/sub | solution.py:421
  (171 shorter events, 43.9 us)
Async XLA Ops:
  7.2 113.5 %all-gather.2.cloned.1.call-start = ((), (), s32[]{:S(2)}) async-start(), calls=%async_computation | async-start | bytes 14868480 | tf_op jit(solution)/shard_map/all_gather | solution.py:460
  13.5 5.4 %collective-permute-start = (bf16[312,128]{1,0:T(8,128)(2,1)S(1)}, bf16[312,128]{1,0:T(8,128)(2,1)S(1)}, u32[]{:S(2)}, u32[]{:S(2)}) collective-permute-start(bf16[312,128]{1,0:T(8,128)(2,1)S(1)} %fusion.31), channel_id=1, source_target_pairs={{0,1},{1,0},{2,3},{3,2},{4,5},{5,4},{6,7},{7,6},{8,9},{9,8},{10,11... | collective-permute-start | bytes 239624 | tf_op jit(solution)/shard_map/ppermute | solution.py:341
  23.7 6.4 %collective-permute-start.2 = (bf16[312,128]{1,0:T(8,128)(2,1)S(1)}, bf16[312,128]{1,0:T(8,128)(2,1)S(1)}, u32[]{:S(2)}, u32[]{:S(2)}) collective-permute-start(bf16[312,128]{1,0:T(8,128)(2,1)S(1)} %add_convert_fusion.9), channel_id=1, source_target_pairs={{0,4},{1,5},{2,6},{3,7},{4,0},{5,1},{6,2},{7,3},{8,12},{9,13},{10,... | collective-permute-start | bytes 239624 | tf_op jit(solution)/shard_map/ppermute | solution.py:341
  30.1 10.1 %collective-permute-start.3 = (bf16[312,128]{1,0:T(8,128)(2,1)S(1)}, bf16[312,128]{1,0:T(8,128)(2,1)S(1)}, u32[]{:S(2)}, u32[]{:S(2)}) collective-permute-start(bf16[312,128]{1,0:T(8,128)(2,1)S(1)} %add_convert_fusion.8), channel_id=1, source_target_pairs={{0,8},{1,9},{2,10},{3,11},{4,12},{5,13},{6,14},{7,15},{8,0},{9,1},... | collective-permute-start | bytes 239624 | tf_op jit(solution)/shard_map/ppermute | solution.py:341
  162.3 16.0 %collective-permute-start.5 = (bf16[768,3072]{1,0:T(8,128)(2,1)}, bf16[768,3072]{1,0:T(8,128)(2,1)}, u32[]{:S(2)}, u32[]{:S(2)}) collective-permute-start(bf16[768,3072]{1,0:T(8,128)(2,1)} %convolution_convert_fusion.1.refs_1_), channel_id=1, source_target_pairs={{0,16},{16,0},{1,17},{17,1},{2,18},{18,2},{3,19},{19,3},{4,20},{20... | collective-permute-start | bytes 14155784 | tf_op jit(solution)/shard_map/ppermute | solution.py:472
  162.6 15.8 %collective-permute-start.6 = (bf16[3072,768]{1,0:T(8,128)(2,1)}, bf16[3072,768]{1,0:T(8,128)(2,1)}, u32[]{:S(2)}, u32[]{:S(2)}) collective-permute-start(bf16[3072,768]{1,0:T(8,128)(2,1)} %convolution_convert_fusion.refs_2_), channel_id=1, source_target_pairs={{0,16},{16,0},{1,17},{17,1},{2,18},{18,2},{3,19},{19,3},{4,20},{20... | collective-permute-start | bytes 14155784 | tf_op jit(solution)/shard_map/ppermute | solution.py:472
  170.2 7.5 %collective-permute-start.4 = (bf16[8,768]{1,0:T(8,128)(2,1)S(1)}, bf16[8,768]{1,0:T(8,128)(2,1)S(1)}, u32[]{:S(2)}, u32[]{:S(2)}) collective-permute-start(bf16[8,768]{1,0:T(8,128)(2,1)S(1)} %maximum_maximum_fusion), channel_id=1, source_target_pairs={{0,16},{16,0},{1,17},{17,1},{2,18},{18,2},{3,19},{19,3},{4,20},{20... | collective-permute-start | bytes 36872 | tf_op jit(solution)/shard_map/ppermute | solution.py:472
  196.9 49.4 %collective-permute-start.8 = (bf16[8,384,128]{2,1,0:T(8,128)(2,1)}, bf16[8,384,128]{2,1,0:T(8,128)(2,1)S(1)}, u32[]{:S(2)}, u32[]{:S(2)}) collective-permute-start(bf16[8,384,128]{2,1,0:T(8,128)(2,1)} %get-tuple-element.77), channel_id=1, source_target_pairs={{0,2},{1,3},{2,0},{3,1},{4,6},{5,7},{6,4},{7,5},{8,10},{9,11},{10,... | collective-permute-start | bytes 2359304 | tf_op jit(solution)/shard_map/ppermute | solution.py:341
  218.6 5.2 %collective-permute-start.7 = (bf16[312,128]{1,0:T(8,128)(2,1)S(1)}, bf16[312,128]{1,0:T(8,128)(2,1)S(1)}, u32[]{:S(2)}, u32[]{:S(2)}) collective-permute-start(bf16[312,128]{1,0:T(8,128)(2,1)S(1)} %reshape.91), channel_id=1, source_target_pairs={{0,16},{16,0},{1,17},{17,1},{2,18},{18,2},{3,19},{19,3},{4,20},{20... | collective-permute-start | bytes 239624 | tf_op jit(solution)/shard_map/ppermute | solution.py:354
  219.3 10.5 %collective-permute-start.30 = (bf16[4,224,128]{2,1,0:T(8,128)(2,1)S(1)}, bf16[4,224,128]{2,1,0:T(8,128)(2,1)S(1)}, u32[]{:S(2)}, u32[]{:S(2)}) collective-permute-start(bf16[4,224,128]{2,1,0:T(8,128)(2,1)S(1)} %copy-done.24), channel_id=1, source_target_pairs={{0,12},{1,13},{2,14},{3,15},{4,8},{5,9},{6,10},{7,11},{8,4},{9,5},... | collective-permute-start | bytes 688136 | tf_op jit(solution)/shard_map/ppermute | solution.py:341
  221.1 21.4 %collective-permute-start.29 = (bf16[4,224,128]{2,1,0:T(8,128)(2,1)S(1)}, bf16[4,224,128]{2,1,0:T(8,128)(2,1)S(1)}, u32[]{:S(2)}, u32[]{:S(2)}) collective-permute-start(bf16[4,224,128]{2,1,0:T(8,128)(2,1)S(1)} %copy-done.23), channel_id=1, source_target_pairs={{0,8},{1,9},{2,10},{3,11},{4,12},{5,13},{6,14},{7,15},{8,0},{9,1},... | collective-permute-start | bytes 688136 | tf_op jit(solution)/shard_map/ppermute | solution.py:341
  221.8 20.7 %collective-permute-start.28 = (bf16[4,224,128]{2,1,0:T(8,128)(2,1)S(1)}, bf16[4,224,128]{2,1,0:T(8,128)(2,1)S(1)}, u32[]{:S(2)}, u32[]{:S(2)}) collective-permute-start(bf16[4,224,128]{2,1,0:T(8,128)(2,1)S(1)} %copy-done.22), channel_id=1, source_target_pairs={{0,4},{1,5},{2,6},{3,7},{4,0},{5,1},{6,2},{7,3},{8,12},{9,13},{10,... | collective-permute-start | bytes 688136 | tf_op jit(solution)/shard_map/ppermute | solution.py:341
  223.8 23.2 %collective-permute-start.9 = (bf16[8,384,128]{2,1,0:T(8,128)(2,1)S(1)}, bf16[8,384,128]{2,1,0:T(8,128)(2,1)S(1)}, u32[]{:S(2)}, u32[]{:S(2)}) collective-permute-start(bf16[8,384,128]{2,1,0:T(8,128)(2,1)S(1)} %copy-done.21), channel_id=1, source_target_pairs={{0,1},{1,0},{2,3},{3,2},{4,5},{5,4},{6,7},{7,6},{8,9},{9,8},{10,11... | collective-permute-start | bytes 2359304 | tf_op jit(solution)/shard_map/ppermute | solution.py:341
  242.7 5.8 %collective-permute-start.33 = (bf16[224,128]{1,0:T(8,128)(2,1)S(1)}, bf16[224,128]{1,0:T(8,128)(2,1)S(1)}, u32[]{:S(2)}, u32[]{:S(2)}) collective-permute-start(bf16[224,128]{1,0:T(8,128)(2,1)S(1)} %get-tuple-element.120), channel_id=1, source_target_pairs={{0,3},{1,2},{2,1},{3,0},{4,7},{5,6},{6,5},{7,4},{8,11},{9,10},{10,... | collective-permute-start | bytes 172040 | tf_op jit(solution)/shard_map/ppermute | solution.py:341
  246.4 12.1 %collective-permute-start.20 = (bf16[4,384,128]{2,1,0:T(8,128)(2,1)S(1)}, bf16[4,384,128]{2,1,0:T(8,128)(2,1)S(1)}, u32[]{:S(2)}, u32[]{:S(2)}) collective-permute-start(bf16[4,384,128]{2,1,0:T(8,128)(2,1)S(1)} %add_convert_fusion.3), channel_id=1, source_target_pairs={{0,1},{1,0},{2,3},{3,2},{4,5},{5,4},{6,7},{7,6},{8,9},{9,8},{10,11... | collective-permute-start | bytes 1179656 | tf_op jit(solution)/shard_map/ppermute | solution.py:341
  247.1 12.1 %collective-permute-start.21 = (bf16[4,384,128]{2,1,0:T(8,128)(2,1)S(1)}, bf16[4,384,128]{2,1,0:T(8,128)(2,1)S(1)}, u32[]{:S(2)}, u32[]{:S(2)}) collective-permute-start(bf16[4,384,128]{2,1,0:T(8,128)(2,1)S(1)} %add_convert_fusion.2), channel_id=1, source_target_pairs={{0,2},{1,3},{2,0},{3,1},{4,6},{5,7},{6,4},{7,5},{8,10},{9,11},{10,... | collective-permute-start | bytes 1179656 | tf_op jit(solution)/shard_map/ppermute | solution.py:341
  249.6 24.3 %collective-permute-start.10 = (bf16[8,384,128]{2,1,0:T(8,128)(2,1)S(1)}, bf16[8,384,128]{2,1,0:T(8,128)(2,1)S(1)}, u32[]{:S(2)}, u32[]{:S(2)}) collective-permute-start(bf16[8,384,128]{2,1,0:T(8,128)(2,1)S(1)} %copy-done.20), channel_id=1, source_target_pairs={{0,2},{1,3},{2,0},{3,1},{4,6},{5,7},{6,4},{7,5},{8,10},{9,11},{10,... | collective-permute-start | bytes 2359304 | tf_op jit(solution)/shard_map/ppermute | solution.py:341
  251.0 24.3 %collective-permute-start.11 = (bf16[8,384,128]{2,1,0:T(8,128)(2,1)S(1)}, bf16[8,384,128]{2,1,0:T(8,128)(2,1)S(1)}, u32[]{:S(2)}, u32[]{:S(2)}) collective-permute-start(bf16[8,384,128]{2,1,0:T(8,128)(2,1)S(1)} %copy-done.19), channel_id=1, source_target_pairs={{0,1},{1,0},{2,3},{3,2},{4,5},{5,4},{6,7},{7,6},{8,9},{9,8},{10,11... | collective-permute-start | bytes 2359304 | tf_op jit(solution)/shard_map/ppermute | solution.py:341
  259.5 16.6 %collective-permute-start.24 = (bf16[768,128]{1,0:T(8,128)(2,1)S(1)}, bf16[768,128]{1,0:T(8,128)(2,1)S(1)}, u32[]{:S(2)}, u32[]{:S(2)}) collective-permute-start(bf16[768,128]{1,0:T(8,128)(2,1)S(1)} %get-tuple-element.114), channel_id=1, source_target_pairs={{0,12},{1,13},{2,14},{3,15},{4,8},{5,9},{6,10},{7,11},{8,4},{9,5},... | collective-permute-start | bytes 589832 | tf_op jit(solution)/shard_map/ppermute | solution.py:341
  261.7 14.4 %collective-permute-start.23 = (bf16[768,128]{1,0:T(8,128)(2,1)S(1)}, bf16[768,128]{1,0:T(8,128)(2,1)S(1)}, u32[]{:S(2)}, u32[]{:S(2)}) collective-permute-start(bf16[768,128]{1,0:T(8,128)(2,1)S(1)} %get-tuple-element.115), channel_id=1, source_target_pairs={{0,8},{1,9},{2,10},{3,11},{4,12},{5,13},{6,14},{7,15},{8,0},{9,1},... | collective-permute-start | bytes 589832 | tf_op jit(solution)/shard_map/ppermute | solution.py:341
  261.7 14.4 %collective-permute-start.22 = (bf16[768,128]{1,0:T(8,128)(2,1)S(1)}, bf16[768,128]{1,0:T(8,128)(2,1)S(1)}, u32[]{:S(2)}, u32[]{:S(2)}) collective-permute-start(bf16[768,128]{1,0:T(8,128)(2,1)S(1)} %get-tuple-element.113), channel_id=1, source_target_pairs={{0,4},{1,5},{2,6},{3,7},{4,0},{5,1},{6,2},{7,3},{8,12},{9,13},{10,... | collective-permute-start | bytes 589832 | tf_op jit(solution)/shard_map/ppermute | solution.py:341
  274.0 10.8 %collective-permute-start.15 = (bf16[4,384,128]{2,1,0:T(8,128)(2,1)S(1)}, bf16[4,384,128]{2,1,0:T(8,128)(2,1)S(1)}, u32[]{:S(2)}, u32[]{:S(2)}) collective-permute-start(bf16[4,384,128]{2,1,0:T(8,128)(2,1)S(1)} %add_convert_fusion.1), channel_id=1, source_target_pairs={{0,1},{1,0},{2,3},{3,2},{4,5},{5,4},{6,7},{7,6},{8,9},{9,8},{10,11... | collective-permute-start | bytes 1179656 | tf_op jit(solution)/shard_map/ppermute | solution.py:341
  275.4 11.0 %collective-permute-start.16 = (bf16[4,384,128]{2,1,0:T(8,128)(2,1)S(1)}, bf16[4,384,128]{2,1,0:T(8,128)(2,1)S(1)}, u32[]{:S(2)}, u32[]{:S(2)}) collective-permute-start(bf16[4,384,128]{2,1,0:T(8,128)(2,1)S(1)} %add_convert_fusion), channel_id=1, source_target_pairs={{0,2},{1,3},{2,0},{3,1},{4,6},{5,7},{6,4},{7,5},{8,10},{9,11},{10,... | collective-permute-start | bytes 1179656 | tf_op jit(solution)/shard_map/ppermute | solution.py:341
  276.3 12.7 %collective-permute-start.14 = (bf16[312,128]{1,0:T(8,128)(2,1)S(1)}, bf16[312,128]{1,0:T(8,128)(2,1)S(1)}, u32[]{:S(2)}, u32[]{:S(2)}) collective-permute-start(bf16[312,128]{1,0:T(8,128)(2,1)S(1)} %add_convert_fusion.6), channel_id=1, source_target_pairs={{0,3},{1,2},{2,1},{3,0},{4,7},{5,6},{6,5},{7,4},{8,11},{9,10},{10,... | collective-permute-start | bytes 239624 | tf_op jit(solution)/shard_map/ppermute | solution.py:341
  278.0 13.2 %collective-permute-start.13 = (bf16[312,128]{1,0:T(8,128)(2,1)S(1)}, bf16[312,128]{1,0:T(8,128)(2,1)S(1)}, u32[]{:S(2)}, u32[]{:S(2)}) collective-permute-start(bf16[312,128]{1,0:T(8,128)(2,1)S(1)} %add_convert_fusion.6), channel_id=1, source_target_pairs={{0,2},{1,3},{2,0},{3,1},{4,6},{5,7},{6,4},{7,5},{8,10},{9,11},{10,... | collective-permute-start | bytes 239624 | tf_op jit(solution)/shard_map/ppermute | solution.py:341
  278.9 12.3 %collective-permute-start.12 = (bf16[312,128]{1,0:T(8,128)(2,1)S(1)}, bf16[312,128]{1,0:T(8,128)(2,1)S(1)}, u32[]{:S(2)}, u32[]{:S(2)}) collective-permute-start(bf16[312,128]{1,0:T(8,128)(2,1)S(1)} %add_convert_fusion.6), channel_id=1, source_target_pairs={{0,1},{1,0},{2,3},{3,2},{4,5},{5,4},{6,7},{7,6},{8,9},{9,8},{10,11... | collective-permute-start | bytes 239624 | tf_op jit(solution)/shard_map/ppermute | solution.py:341
  286.7 9.7 %collective-permute-start.27 = (bf16[768,128]{1,0:T(8,128)(2,1)S(1)}, bf16[768,128]{1,0:T(8,128)(2,1)S(1)}, u32[]{:S(2)}, u32[]{:S(2)}) collective-permute-start(bf16[768,128]{1,0:T(8,128)(2,1)S(1)} %get-tuple-element.117), channel_id=1, source_target_pairs={{0,12},{1,13},{2,14},{3,15},{4,8},{5,9},{6,10},{7,11},{8,4},{9,5},... | collective-permute-start | bytes 589832 | tf_op jit(solution)/shard_map/ppermute | solution.py:341
  288.9 16.6 %collective-permute-start.26 = (bf16[768,128]{1,0:T(8,128)(2,1)S(1)}, bf16[768,128]{1,0:T(8,128)(2,1)S(1)}, u32[]{:S(2)}, u32[]{:S(2)}) collective-permute-start(bf16[768,128]{1,0:T(8,128)(2,1)S(1)} %get-tuple-element.118), channel_id=1, source_target_pairs={{0,8},{1,9},{2,10},{3,11},{4,12},{5,13},{6,14},{7,15},{8,0},{9,1},... | collective-permute-start | bytes 589832 | tf_op jit(solution)/shard_map/ppermute | solution.py:341
  288.9 16.6 %collective-permute-start.25 = (bf16[768,128]{1,0:T(8,128)(2,1)S(1)}, bf16[768,128]{1,0:T(8,128)(2,1)S(1)}, u32[]{:S(2)}, u32[]{:S(2)}) collective-permute-start(bf16[768,128]{1,0:T(8,128)(2,1)S(1)} %get-tuple-element.116), channel_id=1, source_target_pairs={{0,4},{1,5},{2,6},{3,7},{4,0},{5,1},{6,2},{7,3},{8,12},{9,13},{10,... | collective-permute-start | bytes 589832 | tf_op jit(solution)/shard_map/ppermute | solution.py:341
  291.2 15.5 %collective-permute-start.19 = (bf16[312,128]{1,0:T(8,128)(2,1)S(1)}, bf16[312,128]{1,0:T(8,128)(2,1)S(1)}, u32[]{:S(2)}, u32[]{:S(2)}) collective-permute-start(bf16[312,128]{1,0:T(8,128)(2,1)S(1)} %add_convert_fusion.5), channel_id=1, source_target_pairs={{0,12},{1,13},{2,14},{3,15},{4,8},{5,9},{6,10},{7,11},{8,4},{9,5},... | collective-permute-start | bytes 239624 | tf_op jit(solution)/shard_map/ppermute | solution.py:341
  293.4 13.7 %collective-permute-start.18 = (bf16[312,128]{1,0:T(8,128)(2,1)S(1)}, bf16[312,128]{1,0:T(8,128)(2,1)S(1)}, u32[]{:S(2)}, u32[]{:S(2)}) collective-permute-start(bf16[312,128]{1,0:T(8,128)(2,1)S(1)} %add_convert_fusion.5), channel_id=1, source_target_pairs={{0,8},{1,9},{2,10},{3,11},{4,12},{5,13},{6,14},{7,15},{8,0},{9,1},... | collective-permute-start | bytes 239624 | tf_op jit(solution)/shard_map/ppermute | solution.py:341
  296.4 10.8 %collective-permute-start.17 = (bf16[312,128]{1,0:T(8,128)(2,1)S(1)}, bf16[312,128]{1,0:T(8,128)(2,1)S(1)}, u32[]{:S(2)}, u32[]{:S(2)}) collective-permute-start(bf16[312,128]{1,0:T(8,128)(2,1)S(1)} %add_convert_fusion.5), channel_id=1, source_target_pairs={{0,4},{1,5},{2,6},{3,7},{4,0},{5,1},{6,2},{7,3},{8,12},{9,13},{10,... | collective-permute-start | bytes 239624 | tf_op jit(solution)/shard_map/ppermute | solution.py:341
  (33 other events, 544.8 us)
Sparse Core Ops, SparseCore 0:
  11.4 109.2 all-gather.1
